TPU v7x, 32 devices: a whole 2x2x4 slice. The times are simulated.
32 devices in a mesh: seq: 8 (over y, x, core), fsdp: 4 (over z).
Axes of the slice: x: 2, y: 2, z: 4, core: 2. Of those that a mesh axis runs over, the one named last changes fastest.
Arguments:
- tokens: bfloat16 [8192, 768], P(('seq', 'fsdp')), may hold values from -6 to 6
- query_small: bfloat16 [768, 512], P(('seq', 'fsdp')), may hold values from -0.21875 to 0.21875
- key_small: bfloat16 [768, 512], P(('seq', 'fsdp')), may hold values from -0.21875 to 0.21875
- value_small: bfloat16 [768, 512], P(('seq', 'fsdp')), may hold values from -0.21875 to 0.21875
- out_small: bfloat16 [512, 768], P(None, ('seq', 'fsdp')), may hold values from -1.5 to 1.5
- query_large: bfloat16 [768, 768], P(('seq', 'fsdp')), may hold values from -0.21875 to 0.21875
- key_large: bfloat16 [768, 768], P(('seq', 'fsdp')), may hold values from -0.21875 to 0.21875
- value_large: bfloat16 [768, 768], P(('seq', 'fsdp')), may hold values from -0.21875 to 0.21875
- out_large: bfloat16 [768, 768], P(None, ('seq', 'fsdp')), may hold values from -1.25 to 1.25
- attend_gain: bfloat16 [768], P(('seq', 'fsdp')), may hold values from 0.5 to 1.5
- attend_router: bfloat16 [768], P(('seq', 'fsdp')), may hold values from -0.15625 to 0.15625
- gate_small: bfloat16 [768, 1024], P(('seq', 'fsdp')), may hold values from -0.21875 to 0.21875
- up_small: bfloat16 [768, 1024], P(('seq', 'fsdp')), may hold values from -0.21875 to 0.21875
- down_small: bfloat16 [1024, 768], P(None, ('seq', 'fsdp')), may hold values from -0.1875 to 0.1875
- gate_large: bfloat16 [768, 4096], P(('seq', 'fsdp')), may hold values from -0.21875 to 0.21875
- up_large: bfloat16 [768, 4096], P(('seq', 'fsdp')), may hold values from -0.21875 to 0.21875
- down_large: bfloat16 [4096, 768], P(None, ('seq', 'fsdp')), may hold values from -0.09375 to 0.09375
- feed_gain: bfloat16 [768], P(('seq', 'fsdp')), may hold values from 0.5 to 1.5
- feed_router: bfloat16 [768], P(('seq', 'fsdp')), may hold values from -0.15625 to 0.15625
- lengths: int32 [2], replicated, may hold values from 256 to 7936, as said below
- query_route: int32 [32, 32], replicated, may hold values from 0 to 256, as said below
- key_route: int32 [32, 32], replicated, may hold values from 0 to 256, as said below
- feed_route: int32 [32, 32], P(('seq', 'fsdp')), may hold values from 0 to 256, as said below
- cotangent: bfloat16 [8192, 768], P(('seq', 'fsdp')), may hold values from -6 to 6
Outputs:
- result: bfloat16 [8192, 768], P(('seq', 'fsdp'))
- tokens_grad: float32 [8192, 768], P(('seq', 'fsdp'))
- query_small_grad: float32 [768, 512], P(('seq', 'fsdp'))
- key_small_grad: float32 [768, 512], P(('seq', 'fsdp'))
- value_small_grad: float32 [768, 512], P(('seq', 'fsdp'))
- out_small_grad: float32 [512, 768], P(None, ('seq', 'fsdp'))
- query_large_grad: float32 [768, 768], P(('seq', 'fsdp'))
- key_large_grad: float32 [768, 768], P(('seq', 'fsdp'))
- value_large_grad: float32 [768, 768], P(('seq', 'fsdp'))
- out_large_grad: float32 [768, 768], P(None, ('seq', 'fsdp'))
- attend_gain_grad: float32 [768], P(('seq', 'fsdp'))
- attend_router_grad: float32 [768], P(('seq', 'fsdp'))
- gate_small_grad: float32 [768, 1024], P(('seq', 'fsdp'))
- up_small_grad: float32 [768, 1024], P(('seq', 'fsdp'))
- down_small_grad: float32 [1024, 768], P(None, ('seq', 'fsdp'))
- gate_large_grad: float32 [768, 4096], P(('seq', 'fsdp'))
- up_large_grad: float32 [768, 4096], P(('seq', 'fsdp'))
- down_large_grad: float32 [4096, 768], P(None, ('seq', 'fsdp'))
- feed_gain_grad: float32 [768], P(('seq', 'fsdp'))
- feed_router_grad: float32 [768], P(('seq', 'fsdp'))
Inputs may be any that keep to these rules, and one draw needn't show every extreme that they name: `lengths`: entry 1 (the short document) lies between 256 and 512; both entries together leave at most 128 padding tokens at the end of the pack. `query_route`: row b lists distinct live positions inside aligned block b of 256 tokens, filled slots first and 256 in empty ones; every block with a live token has at least one; in every draw some block fills all 32. `key_route`: row b lists distinct live positions inside aligned block b of 256 tokens, filled slots first and 256 in empty ones; every block with a live token has at least one; in every draw some block fills all 32. `feed_route`: row b lists distinct live positions inside aligned block b of 256 tokens, filled slots first and 256 in empty ones; every block with a live token has at least one; in every draw some block fills all 32.
All inputs are finite; a program needn't handle non-finite values.
Results may differ from a plain program's by a relative error of at most 0.014.
Values may be sent and summed in bfloat16 or wider, within the bound.
No kernel may reach another device: no remote copies, remote signals or barrier semaphores. Data moves between devices by JAX's collectives and lax.ppermute only.
A program may use at most 256 MiB of HBM per device.

v0:
```python
import math

import jax
import jax.numpy as jnp
from jax import lax
from jax.sharding import PartitionSpec as P

HL = 8
HDL = 64
HH = 12
HDH = 64
RADIUS = 128

NEG = -1e30
EPS = 1e-06
HIGH = lax.Precision.HIGHEST
AXES = ("seq", "fsdp")
F32 = jnp.float32
BF16 = jnp.bfloat16


def dot(left, right, dims):
    return lax.dot_general(left, right, (dims, ((), ())), preferred_element_type=F32)


def nn(left, right):
    return dot(left, right, ((1,), (0,)))


def nt(left, right):
    return dot(left, right, ((1,), (1,)))


def tn(left, right):
    return dot(left, right, ((0,), (0,)))


def reverse_bits(value, count):
    out = value * 0
    for j in range(count):
        out = out | (((value >> j) & 1) << (count - 1 - j))
    return out


class Net:
    def __init__(self):
        self.seq = lax.axis_size("seq")
        self.depth = lax.axis_size("fsdp")
        self.levels = (self.seq // 2).bit_length() - 1
        self.count = self.seq * self.depth
        s = lax.axis_index("seq")
        self.core, self.pair = s & 1, s >> 1
        self.z = lax.axis_index("fsdp")
        self.device = s * self.depth + self.z

    def pairs(self, move):
        out = []
        for s in range(self.seq):
            for z in range(self.depth):
                pair, core, to_z = move(s >> 1, s & 1, z)
                out.append((s * self.depth + z, (pair * 2 + core) * self.depth + to_z))
        return out

    def by_core(self, array):
        return lax.ppermute(array, AXES, self.pairs(lambda p, c, z: (p, 1 - c, z)))

    def by_bit(self, array, j):
        top = self.levels - 1 - j
        return lax.ppermute(
            array, AXES, self.pairs(lambda p, c, z: (p ^ (1 << (j if c else top)), c, z))
        )

    def by_z(self, array, k):
        return lax.ppermute(array, AXES, self.pairs(lambda p, c, z: (p, c, z ^ k)))

    def target(self, relative):
        zr = relative % self.depth
        bits = (relative // self.depth) % (self.seq // 2)
        core = self.core ^ (relative // (self.count // 2))
        pair = self.pair ^ jnp.where(core == 1, bits, reverse_bits(bits, self.levels))
        return (pair * 2 + core) * self.depth + (self.z ^ zr)

    def gather_z(self, shard):
        return jnp.concatenate([shard] + [self.by_z(shard, k) for k in range(1, self.depth)], axis=0)

    def gather_seq(self, shard):
        for j in range(self.levels):
            shard = jnp.concatenate([shard, self.by_bit(shard, j)], axis=0)
        return shard, self.by_core(shard)

    def gather(self, shard):
        return self.gather_seq(self.gather_z(shard))

    def reduce_seq(self, keep, send):
        total = keep + self.by_core(send.astype(BF16)).astype(F32)
        for j in reversed(range(self.levels)):
            half = total.shape[0] // 2
            moved = self.by_bit(total[half:].astype(BF16), j)
            total = total[:half] + moved.astype(F32)
        return total

    def reduce_z(self, total):
        width = total.shape[0] // self.depth
        out = total[:width]
        for k in range(1, self.depth):
            part = total[k * width : (k + 1) * width].astype(BF16)
            out = out + self.by_z(part, k).astype(F32)
        return out

    def reduce(self, keep, send):
        return self.reduce_z(self.reduce_seq(keep, send))


def unit_rms(values):
    scale = lax.rsqrt(jnp.mean(values * values, -1, keepdims=True) + EPS)
    return values * scale, scale


def norm_back(grad, gain, unit, scale):
    scaled = grad * gain
    return scale * (scaled - unit * jnp.mean(scaled * unit, -1, keepdims=True))


def geglu(gate, upper):
    return jax.nn.gelu(gate, approximate=True) * upper


def document_of(places, lengths):
    return (places >= lengths[0]).astype(jnp.int32)


def local_mask(query_pos, key_pos, lengths, total):
    inside = (key_pos >= 0) & (key_pos < total)
    live_end = lengths[0] + lengths[1]
    live_query = query_pos < live_end
    live_key = inside & (key_pos < live_end)
    same = document_of(query_pos, lengths)[:, None] == document_of(key_pos, lengths)[None, :]
    near = jnp.abs(query_pos[:, None] - key_pos[None, :]) <= RADIUS
    both = live_query[:, None] & live_key[None, :] | (query_pos[:, None] == key_pos[None, :])
    return near & inside[None, :] & same & both


def one_hot(route_row, rows):
    return (route_row[:, None] == jnp.arange(rows, dtype=jnp.int32)[None, :]).astype(BF16)


def spread(select, values):
    return lax.dot_general(
        select.astype(F32),
        values,
        (((0,), (0,)), ((), ())),
        precision=HIGH,
        preferred_element_type=F32,
    )


def pick_wide(select, values):
    return jnp.dot(select.astype(F32), values, precision=HIGH, preferred_element_type=F32)


def soft(scores):
    top = jnp.max(scores, -1, keepdims=True)
    expo = jnp.exp(scores - top)
    return expo / jnp.sum(expo, -1, keepdims=True)


def reorder_wide(values, order):
    high = values.astype(BF16)
    low = (values - high.astype(F32)).astype(BF16)
    return nn(high, order) + nn(low, order)


def per_device(
    tokens,
    query_small,
    key_small,
    value_small,
    out_small,
    query_large,
    key_large,
    value_large,
    out_large,
    attend_gain,
    attend_router,
    gate_small,
    up_small,
    down_small,
    gate_large,
    up_large,
    down_large,
    feed_gain,
    feed_router,
    lengths,
    query_route,
    key_route,
    feed_route,
    cotangent,
):
    net = Net()
    rows, width = tokens.shape
    blocks = net.count
    part = width // blocks
    half = width // 2
    total = rows * blocks
    first = net.device * rows
    light = HL * HDL
    heavy = HH * HDH
    narrow = down_small.shape[0]
    wide = down_large.shape[0]
    light_scale = 1.0 / math.sqrt(HDL)
    heavy_scale = 1.0 / math.sqrt(HDH)

    step = [(i, i + 1) for i in range(blocks - 1)]
    back = [(i + 1, i) for i in range(blocks - 1)]
    above = lax.ppermute(tokens[rows - RADIUS :], AXES, step)
    below = lax.ppermute(tokens[:RADIUS], AXES, back)
    own_keys = lax.dynamic_slice_in_dim(key_route, net.device, 1, 0)[0]
    own_queries = lax.dynamic_slice_in_dim(query_route, net.device, 1, 0)[0]
    key_select = one_hot(own_keys, rows)
    query_select = one_hot(own_queries, rows)
    feed_select = one_hot(feed_route[0], rows)
    keyed_raw = nn(key_select, tokens).astype(BF16)
    keyed_raw = lax.all_gather(keyed_raw, AXES, axis=0, tiled=True)

    vectors = jnp.stack([attend_gain, attend_router, feed_gain, feed_router], axis=1)
    vectors = jnp.pad(vectors, ((0, 0), (0, 124)))
    first_set = net.gather(
        jnp.concatenate([query_small, key_small, value_small, vectors], axis=1)
    )
    second_set = net.gather(
        jnp.concatenate(
            [query_large, key_large, value_large, out_large.T, out_small.T], axis=1
        )
    )
    third_set = net.gather(jnp.concatenate([gate_small, up_small, down_small.T], axis=1))

    share = wide // net.seq
    stacked = jnp.stack([gate_large, up_large, down_large.T], axis=0)
    stacked = stacked.reshape(3, part, net.seq, share).transpose(2, 1, 0, 3)
    stacked = stacked.reshape(net.seq, part, 3 * share)
    stacked = lax.all_to_all(stacked, "seq", 0, 0, tiled=True)
    expert = net.gather_z(stacked.reshape(net.seq * part, 3 * share))
    gate_slice = expert[:, :share]
    up_slice = expert[:, share : 2 * share]
    down_slice = expert[:, 2 * share :]

    column = jnp.arange(width, dtype=jnp.int32)
    own_order = net.target(column // part) * part + column % part
    group = column // part
    group_order = (group % net.seq) * net.depth + (net.z ^ (group // net.seq))
    group_order = group_order * part + column % part
    to_own = (column[:, None] == own_order[None, :]).astype(BF16)
    own_to_group = (own_order[:, None] == group_order[None, :]).astype(BF16)

    ext = jnp.concatenate([above, tokens, below], axis=0)
    ext_raw = nn(ext, to_own)
    keyed_mine = nn(keyed_raw, to_own)
    cot = nn(cotangent, to_own).astype(BF16)

    def halves(pack, lo, hi):
        return pack[0][:, lo:hi], pack[1][:, lo:hi]

    def into(values, pack):
        return nn(values[:, :half], pack[0]) + nn(values[:, half:], pack[1])

    def onto(values, pack):
        return jnp.concatenate([nt(values, pack[0]), nt(values, pack[1])], axis=1)

    vector_rows = jnp.concatenate(halves(first_set, 3 * light, 3 * light + 8), axis=0)
    vector_rows = vector_rows.T.astype(F32)
    gain_one, router_one, gain_two, router_two = (vector_rows[i : i + 1] for i in range(4))

    unit_ext, scale_ext = unit_rms(ext_raw)
    normed_ext = (unit_ext * gain_one).astype(BF16)
    unit_one, scale_one = unit_ext[RADIUS : RADIUS + rows], scale_ext[RADIUS : RADIUS + rows]
    normed_one = normed_ext[RADIUS : RADIUS + rows]
    inputs = ext_raw[RADIUS : RADIUS + rows]
    unit_key, unused_scale = unit_rms(keyed_mine)
    keyed_rows = (unit_key * gain_one).astype(BF16)

    w_query = halves(first_set, 0, light)
    w_pair = halves(first_set, light, 3 * light)
    w_query_large = halves(second_set, 0, heavy)
    w_pair_large = halves(second_set, heavy, 3 * heavy)
    w_out_large = halves(second_set, 3 * heavy, 4 * heavy)
    w_out = halves(second_set, 4 * heavy, 4 * heavy + light)
    w_gate_up = halves(third_set, 0, 2 * narrow)
    w_down = halves(third_set, 2 * narrow, 3 * narrow)

    query_rows = into(normed_one, w_query).astype(BF16)
    pair_rows = into(normed_ext, w_pair).astype(BF16)
    positions = first + jnp.arange(rows, dtype=jnp.int32)
    key_positions = first - RADIUS + jnp.arange(rows + 2 * RADIUS, dtype=jnp.int32)
    light_mask = local_mask(positions, key_positions, lengths, total)
    query_heads = query_rows.reshape(rows, HL, HDL)
    key_heads = pair_rows[:, :light].reshape(-1, HL, HDL)
    value_heads = pair_rows[:, light:].reshape(-1, HL, HDL)

    def per_head(pattern, left, right):
        return jnp.einsum(pattern, left, right, preferred_element_type=F32)

    light_scores = per_head("qhd,khd->hqk", query_heads, key_heads) * light_scale
    light_probs = soft(jnp.where(light_mask[None], light_scores, NEG))
    light_low = light_probs.astype(BF16)
    light_mixed = per_head("hqk,khd->qhd", light_low, value_heads)
    light_mixed = light_mixed.reshape(rows, light).astype(BF16)
    light_branch = onto(light_mixed, w_out)

    routed_rows = nn(query_select, normed_one).astype(BF16)
    attend_score = jax.nn.sigmoid(jnp.sum(routed_rows.astype(F32) * router_one, -1, keepdims=True))
    routed_query = into(routed_rows, w_query_large).astype(BF16)
    heavy_pair = into(keyed_rows, w_pair_large).astype(BF16)
    key_slots = (jnp.arange(blocks, dtype=jnp.int32)[:, None] * rows + key_route).reshape(-1)
    key_valid = (key_route < rows).reshape(-1)
    key_docs = document_of(key_slots, lengths)
    query_docs = document_of(first + own_queries, lengths)
    heavy_mask = (query_docs[:, None] == key_docs[None, :]) & key_valid[None, :]
    routed_heads = routed_query.reshape(-1, HH, HDH)
    heavy_keys = heavy_pair[:, :heavy].reshape(-1, HH, HDH)
    heavy_values = heavy_pair[:, heavy:].reshape(-1, HH, HDH)
    heavy_scores = per_head("qhd,khd->hqk", routed_heads, heavy_keys) * heavy_scale
    heavy_probs = soft(jnp.where(heavy_mask[None], heavy_scores, NEG))
    heavy_low = heavy_probs.astype(BF16)
    heavy_mixed = per_head("hqk,khd->qhd", heavy_low, heavy_values)
    heavy_mixed = heavy_mixed.reshape(-1, heavy).astype(BF16)
    heavy_branch = onto(heavy_mixed, w_out_large)
    middle = inputs + light_branch + spread(query_select, attend_score * heavy_branch)

    unit_two, scale_two = unit_rms(middle)
    normed_two = (unit_two * gain_two).astype(BF16)
    feed_rows = nn(feed_select, normed_two).astype(BF16)
    feed_grad_rows = nn(feed_select, cot)
    feed_score = jax.nn.sigmoid(jnp.sum(feed_rows.astype(F32) * router_two, -1, keepdims=True))
    grad_feed_heavy = (feed_score * feed_grad_rows).astype(BF16)
    slots = feed_rows.shape[0]
    sent = nn(jnp.concatenate([feed_rows, grad_feed_heavy], axis=0), own_to_group).astype(BF16)
    sent = jnp.concatenate([sent[:slots], sent[slots:]], axis=1)
    got = jnp.concatenate(net.gather_seq(sent), axis=0)
    all_rows, all_grads = got[:, :width], got[:, width:]

    gate_up = into(normed_two, w_gate_up)
    gate_light, upper_light = gate_up[:, :narrow], gate_up[:, narrow:]
    hidden_f, light_pull = jax.vjp(geglu, gate_light, upper_light)
    hidden_light = hidden_f.astype(BF16)
    feed_light = onto(hidden_light, w_down)

    gate_heavy, upper_heavy = nn(all_rows, gate_slice), nn(all_rows, up_slice)
    hidden_hf, heavy_pull = jax.vjp(geglu, gate_heavy, upper_heavy)
    hidden_heavy = hidden_hf.astype(BF16)
    grad_gate_hf, grad_upper_hf = heavy_pull(nn(all_grads, down_slice))
    grad_gate_heavy = grad_gate_hf.astype(BF16)
    grad_upper_heavy = grad_upper_hf.astype(BF16)
    partial = jnp.concatenate(
        [
            nt(hidden_heavy, down_slice),
            nt(grad_gate_heavy, gate_slice) + nt(grad_upper_heavy, up_slice),
        ],
        axis=1,
    )
    kept = partial.shape[0] // 2
    summed = net.reduce_seq(partial[:kept], partial[kept:])
    expert_grad = jnp.concatenate(
        [
            tn(all_rows, grad_gate_heavy),
            tn(all_rows, grad_upper_heavy),
            tn(all_grads, hidden_heavy),
        ],
        axis=1,
    )
    expert_grad = net.reduce_z(expert_grad).astype(BF16)
    expert_grad = expert_grad.reshape(net.seq, part, 3 * share)
    expert_grad = lax.all_to_all(expert_grad, "seq", 0, 0, tiled=True)
    expert_grad = expert_grad.reshape(net.seq, part, 3, share).transpose(2, 1, 0, 3)
    expert_grad = expert_grad.reshape(3, part, wide).astype(F32)

    group_to_own = (group_order[:, None] == own_order[None, :]).astype(BF16)
    summed = reorder_wide(
        jnp.concatenate([summed[:, :width], summed[:, width:]], axis=0), group_to_own
    )
    feed_heavy, grad_feed_rows = summed[:slots], summed[slots:]
    result = middle + feed_light + spread(feed_select, feed_score * feed_heavy)
    result = nt(result.astype(BF16), to_own).astype(BF16)

    grad_result = cot.astype(F32)
    grad_gate_f, grad_upper_f = light_pull(into(cot, w_down))
    grad_gate_up = jnp.concatenate([grad_gate_f.astype(BF16), grad_upper_f.astype(BF16)], axis=1)

    def weight_grad(left, right):
        return tn(left[:, :half], right), tn(left[:, half:], right).astype(BF16)

    def beside(*parts):
        return tuple(jnp.concatenate(side, axis=1) for side in zip(*parts))

    third_grad = net.reduce(
        *beside(weight_grad(normed_two, grad_gate_up), weight_grad(cot, hidden_light))
    )
    feed_logit_grad = jnp.sum(feed_grad_rows * feed_heavy, -1, keepdims=True)
    feed_logit_grad = feed_logit_grad * feed_score * (1.0 - feed_score)
    grad_feed_rows = grad_feed_rows + feed_logit_grad * router_two
    grad_router_two = jnp.sum(feed_rows.astype(F32) * feed_logit_grad, 0)
    grad_normed_two = onto(grad_gate_up, w_gate_up) + spread(feed_select, grad_feed_rows)
    grad_gain_two = jnp.sum(grad_normed_two * unit_two, 0)
    grad_middle = grad_result + norm_back(grad_normed_two, gain_two, unit_two, scale_two)

    grad_middle_low = grad_middle.astype(BF16)
    attend_grad_rows = pick_wide(query_select, grad_middle)
    grad_heavy_branch = (attend_score * attend_grad_rows).astype(BF16)
    attend_logit_grad = jnp.sum(attend_grad_rows * heavy_branch, -1, keepdims=True)
    attend_logit_grad = attend_logit_grad * attend_score * (1.0 - attend_score)
    grad_heavy_mixed = into(grad_heavy_branch, w_out_large).astype(BF16)
    grad_heavy_heads = grad_heavy_mixed.reshape(-1, HH, HDH)
    grad_heavy_probs = per_head("qhd,khd->hqk", grad_heavy_heads, heavy_values)
    heavy_delta = jnp.sum(heavy_probs * grad_heavy_probs, -1, keepdims=True)
    grad_heavy_scores = (heavy_probs * (grad_heavy_probs - heavy_delta)).astype(BF16)
    grad_routed_query = per_head("hqk,khd->qhd", grad_heavy_scores, heavy_keys) * heavy_scale
    grad_routed_query = grad_routed_query.reshape(-1, heavy).astype(BF16)
    grad_keys = per_head("hqk,qhd->khd", grad_heavy_scores, routed_heads) * heavy_scale
    grad_values = per_head("hqk,qhd->khd", heavy_low, grad_heavy_heads)
    grad_heavy_pair = jnp.concatenate(
        [grad_keys.reshape(-1, heavy).astype(BF16), grad_values.reshape(-1, heavy).astype(BF16)],
        axis=1,
    )
    grad_routed = onto(grad_routed_query, w_query_large) + attend_logit_grad * router_one
    grad_router_one = jnp.sum(routed_rows.astype(F32) * attend_logit_grad, 0)
    grad_keyed = onto(grad_heavy_pair, w_pair_large)
    key_gain_grad = jnp.sum(grad_keyed * unit_key, 0)
    grad_keyed_low = nt(grad_keyed.astype(BF16), to_own)
    relative = net.target(jnp.arange(blocks, dtype=jnp.int32))
    per_block = grad_keyed_low.astype(BF16).reshape(blocks, -1, width)
    per_block = jnp.take(per_block, relative, axis=0)
    capacity = per_block.shape[1]
    per_block = per_block.reshape(blocks * capacity, width)
    cut = blocks * capacity // 2
    grad_keyed_own = net.reduce(per_block[:cut].astype(F32), per_block[cut:])

    grad_light_mixed = into(grad_middle_low, w_out).astype(BF16)
    second_grad = net.reduce(
        *beside(
            weight_grad(routed_rows, grad_routed_query),
            weight_grad(keyed_rows, grad_heavy_pair),
            weight_grad(grad_heavy_branch, heavy_mixed),
            weight_grad(grad_middle_low, light_mixed),
        )
    )
    grad_light_heads = grad_light_mixed.reshape(rows, HL, HDL)
    grad_light_probs = per_head("qhd,khd->hqk", grad_light_heads, value_heads)
    light_delta = jnp.sum(light_probs * grad_light_probs, -1, keepdims=True)
    grad_light_scores = (light_probs * (grad_light_probs - light_delta)).astype(BF16)
    grad_query_rows = per_head("hqk,khd->qhd", grad_light_scores, key_heads) * light_scale
    grad_query_rows = grad_query_rows.reshape(rows, light).astype(BF16)
    grad_key_ext = per_head("hqk,qhd->khd", grad_light_scores, query_heads) * light_scale
    grad_value_ext = per_head("hqk,qhd->khd", light_low, grad_light_heads)
    grad_pair = jnp.concatenate(
        [
            grad_key_ext.reshape(-1, light).astype(BF16),
            grad_value_ext.reshape(-1, light).astype(BF16),
        ],
        axis=1,
    )
    grad_ext = onto(grad_pair, w_pair)
    outer = jnp.concatenate([grad_ext[:RADIUS], grad_ext[RADIUS + rows :]], axis=0)
    outer = nt(outer.astype(BF16), to_own).astype(BF16)
    from_next = lax.ppermute(outer[:RADIUS], AXES, back)
    from_prev = lax.ppermute(outer[RADIUS:], AXES, step)
    grad_mine = (
        grad_ext[RADIUS : RADIUS + rows]
        + onto(grad_query_rows, w_query)
        + spread(query_select, grad_routed)
    )
    grad_gain_one = (
        jnp.sum(grad_mine * unit_one, 0)
        + jnp.sum(grad_ext[:RADIUS] * unit_ext[:RADIUS], 0)
        + jnp.sum(grad_ext[RADIUS + rows :] * unit_ext[RADIUS + rows :], 0)
        + key_gain_grad
    )
    vector_grads = jnp.stack([grad_gain_one, grad_router_one, grad_gain_two, grad_router_two], 1)
    vector_grads = jnp.pad(vector_grads, ((0, 0), (0, 124)))
    first_grad = net.reduce(
        *beside(
            weight_grad(normed_one, grad_query_rows),
            weight_grad(normed_ext, grad_pair),
            (vector_grads[:half], vector_grads[half:].astype(BF16)),
        )
    )

    arrived = jnp.concatenate([from_prev, from_next, grad_keyed_own.astype(BF16)], axis=0)
    arrived = nn(arrived, to_own)
    grad_normed_one = (
        grad_mine
        + jnp.pad(arrived[:RADIUS], ((0, rows - RADIUS), (0, 0)))
        + jnp.pad(arrived[RADIUS : 2 * RADIUS], ((rows - RADIUS, 0), (0, 0)))
        + spread(key_select, arrived[2 * RADIUS :])
    )
    grad_inputs = grad_middle + norm_back(grad_normed_one, gain_one, unit_one, scale_one)
    back_order = (own_order[:, None] == column[None, :]).astype(BF16)
    tokens_grad = reorder_wide(grad_inputs, back_order)

    vector_out = first_grad[:, 3 * light : 3 * light + 4].T
    return (
        result,
        tokens_grad,
        first_grad[:, :light],
        first_grad[:, light : 2 * light],
        first_grad[:, 2 * light : 3 * light],
        second_grad[:, 4 * heavy :].T,
        second_grad[:, :heavy],
        second_grad[:, heavy : 2 * heavy],
        second_grad[:, 2 * heavy : 3 * heavy],
        second_grad[:, 3 * heavy : 4 * heavy].T,
        vector_out[0],
        vector_out[1],
        third_grad[:, :narrow],
        third_grad[:, narrow : 2 * narrow],
        third_grad[:, 2 * narrow :].T,
        expert_grad[0],
        expert_grad[1],
        expert_grad[2].T,
        vector_out[2],
        vector_out[3],
    )


def solution(mesh):
    by_rows = P(AXES, None)
    by_columns = P(None, AXES)
    vector = P(AXES)
    return jax.shard_map(
        per_device,
        mesh=mesh,
        in_specs=(
            by_rows,
            by_rows,
            by_rows,
            by_rows,
            by_columns,
            by_rows,
            by_rows,
            by_rows,
            by_columns,
            vector,
            vector,
            by_rows,
            by_rows,
            by_columns,
            by_rows,
            by_rows,
            by_columns,
            vector,
            vector,
            P(),
            P(),
            P(),
            by_rows,
            by_rows,
        ),
        out_specs=(
            by_rows,
            by_rows,
            by_rows,
            by_rows,
            by_rows,
            by_columns,
            by_rows,
            by_rows,
            by_rows,
            by_columns,
            vector,
            vector,
            by_rows,
            by_rows,
            by_columns,
            by_rows,
            by_rows,
            by_columns,
            vector,
            vector,
        ),
        check_vma=False,
    )
```

profile of v0, /device:TPU:0, one launch (start us, length us, event | category | flops | bytes accessed | tf_op | source)
XLA Modules:
  0.0 509.6 jit_solution(639047007790402370)
XLA Ops:
  14.4 3.0 collective-permute-start.8
  23.2 3.5 collective-permute-start.3
  34.3 3.9 all-to-all-start
  51.2 6.0 %collective-permute-done.4 = bf16[24,1664]{1,0:T(8,128)(2,1)S(1)} collective-permute-done((bf16[24,1664]{1,0:T(8,128)(2,1)}, bf16[24,1664]{1,0:T(8,128)(2,1)S(1)}, u32[]{:S(2)}, u32[]{:S(2)}) %collective-permute-start.4) | collective-permute-done | bytes 79904 | tf_op jit(solution)/shard_map/ppermute | solution.py:74
  63.1 8.4 %collective-permute-done.15 = bf16[24,3072]{1,0:T(8,128)(2,1)S(1)} collective-permute-done((bf16[24,3072]{1,0:T(8,128)(2,1)S(1)}, bf16[24,3072]{1,0:T(8,128)(2,1)S(1)}, u32[]{:S(2)}, u32[]{:S(2)}) %collective-permute-start.15) | collective-permute-done | bytes 147488 | tf_op jit(solution)/shard_map/ppermute | solution.py:74
  72.8 5.4 %collective-permute-start = (bf16[128,768]{1,0:T(8,128)(2,1)}, bf16[128,768]{1,0:T(8,128)(2,1)}, u32[]{:S(2)}, u32[]{:S(2)}) collective-permute-start(bf16[128,768]{1,0:T(8,128)(2,1)} %get-tuple-element.79), channel_id=1, source_target_pairs={{0,1},{1,2},{2,3},{3,4},{4,5},{5,6},{6,7},{7,8},{8,9},{9,10},{10,1... | collective-permute-start | bytes 589832 | tf_op jit(solution)/shard_map/ppermute | solution.py:215
  91.2 7.6 %collective-permute-done.17 = bf16[96,3072]{1,0:T(8,128)(2,1)} collective-permute-done((bf16[96,3072]{1,0:T(8,128)(2,1)}, bf16[96,3072]{1,0:T(8,128)(2,1)}, u32[]{:S(2)}, u32[]{:S(2)}) %collective-permute-start.17) | collective-permute-done | bytes 589856 | tf_op jit(solution)/shard_map/ppermute | solution.py:69
  101.0 7.2 %collective-permute-done.11 = bf16[96,3584]{1,0:T(8,128)(2,1)S(1)} collective-permute-done((bf16[96,3584]{1,0:T(8,128)(2,1)S(1)}, bf16[96,3584]{1,0:T(8,128)(2,1)S(1)}, u32[]{:S(2)}, u32[]{:S(2)}) %collective-permute-start.11) | collective-permute-done | bytes 688160 | tf_op jit(solution)/shard_map/ppermute | solution.py:69
  120.3 23.1 %collective-permute-done.24 = bf16[192,1536]{1,0:T(8,128)(2,1)} collective-permute-done((bf16[192,1536]{1,0:T(8,128)(2,1)S(1)}, bf16[192,1536]{1,0:T(8,128)(2,1)}, u32[]{:S(2)}, u32[]{:S(2)}) %collective-permute-start.24) | collective-permute-done | bytes 589856 | tf_op jit(solution)/shard_map/ppermute | solution.py:74
  143.3 3.0 pad_maximum_fusion.4
  162.7 3.6 fusion.360
  166.4 3.0 convolution_convert_fusion.10
  176.3 3.1 fusion.112
  179.4 3.0 fusion.83
  182.5 3.1 add_convert_fusion
  197.0 3.1 fusion.68
  249.2 3.9 collective-permute-done.27
  255.0 5.9 %collective-permute-done.57 = bf16[192,1536]{1,0:T(8,128)(2,1)S(1)} collective-permute-done((bf16[192,1536]{1,0:T(8,128)(2,1)S(1)}, bf16[192,1536]{1,0:T(8,128)(2,1)S(1)}, u32[]{:S(2)}, u32[]{:S(2)}) %collective-permute-start.57) | collective-permute-done | bytes 589856 | tf_op jit(solution)/shard_map/ppermute | solution.py:74
  260.9 34.0 %collective-permute-done.56 = bf16[192,1536]{1,0:T(8,128)(2,1)S(1)} collective-permute-done((bf16[192,1536]{1,0:T(8,128)(2,1)S(1)}, bf16[192,1536]{1,0:T(8,128)(2,1)S(1)}, u32[]{:S(2)}, u32[]{:S(2)}) %collective-permute-start.56) | collective-permute-done | bytes 589856 | tf_op jit(solution)/shard_map/ppermute | solution.py:74
  296.1 4.2 all-to-all-start.1
  310.3 3.8 convolution_convert_fusion.7
  323.1 4.1 convolution_convert_fusion.2
  331.6 3.7 fusion.85
  335.3 3.1 fusion.81
  380.7 5.3 %collective-permute-start.29 = (bf16[128,768]{1,0:T(8,128)(2,1)}, bf16[128,768]{1,0:T(8,128)(2,1)}, u32[]{:S(2)}, u32[]{:S(2)}) collective-permute-start(bf16[128,768]{1,0:T(8,128)(2,1)} %get-tuple-element.77), channel_id=1, source_target_pairs={{0,1},{1,2},{2,3},{3,4},{4,5},{5,6},{6,7},{7,8},{8,9},{9,10},{10,1... | collective-permute-start | bytes 589832 | tf_op jit(solution)/shard_map/ppermute | solution.py:464
  396.7 3.0 reshape.866
  425.4 6.7 %collective-permute-done.50 = bf16[192,3072]{1,0:T(8,128)(2,1)} collective-permute-done((bf16[192,3072]{1,0:T(8,128)(2,1)}, bf16[192,3072]{1,0:T(8,128)(2,1)}, u32[]{:S(2)}, u32[]{:S(2)}) %collective-permute-start.50) | collective-permute-done | bytes 1179680 | tf_op jit(solution)/shard_map/ppermute | solution.py:69
  436.3 13.8 %collective-permute-done.51 = bf16[96,3072]{1,0:T(8,128)(2,1)S(1)} collective-permute-done((bf16[96,3072]{1,0:T(8,128)(2,1)S(1)}, bf16[96,3072]{1,0:T(8,128)(2,1)S(1)}, u32[]{:S(2)}, u32[]{:S(2)}) %collective-permute-start.51) | collective-permute-done | bytes 589856 | tf_op jit(solution)/shard_map/ppermute | solution.py:69
  462.2 6.0 %collective-permute-done.39 = bf16[96,1664]{1,0:T(8,128)(2,1)S(1)} collective-permute-done((bf16[96,1664]{1,0:T(8,128)(2,1)S(1)}, bf16[96,1664]{1,0:T(8,128)(2,1)S(1)}, u32[]{:S(2)}, u32[]{:S(2)}) %collective-permute-start.39) | collective-permute-done | bytes 319520 | tf_op jit(solution)/shard_map/ppermute | solution.py:69
  477.8 8.9 %collective-permute-done.45 = bf16[96,3584]{1,0:T(8,128)(2,1)S(1)} collective-permute-done((bf16[96,3584]{1,0:T(8,128)(2,1)S(1)}, bf16[96,3584]{1,0:T(8,128)(2,1)S(1)}, u32[]{:S(2)}, u32[]{:S(2)}) %collective-permute-start.45) | collective-permute-done | bytes 688160 | tf_op jit(solution)/shard_map/ppermute | solution.py:69
  492.1 3.4 collective-permute-done.48
  495.5 5.6 %collective-permute-done.47 = bf16[24,3584]{1,0:T(8,128)(2,1)S(1)} collective-permute-done((bf16[24,3584]{1,0:T(8,128)(2,1)S(1)}, bf16[24,3584]{1,0:T(8,128)(2,1)S(1)}, u32[]{:S(2)}, u32[]{:S(2)}) %collective-permute-start.47) | collective-permute-done | bytes 172064 | tf_op jit(solution)/shard_map/ppermute | solution.py:74
  (647 shorter events, 286.3 us)
Async XLA Ops:
  7.2 164.4 %all-gather.2.cloned.1.call-start = ((), (), s32[]{:S(2)}) async-start(), calls=%async_computation.2 | async-start | bytes 1622016 | tf_op jit(solution)/shard_map/all_gather | solution.py:223
  14.4 66.0 %collective-permute-start.8 = (bf16[24,3584]{1,0:T(8,128)(2,1)}, bf16[24,3584]{1,0:T(8,128)(2,1)S(1)}, u32[]{:S(2)}, u32[]{:S(2)}) collective-permute-start(bf16[24,3584]{1,0:T(8,128)(2,1)} %get-tuple-element.143), channel_id=1, source_target_pairs={{0,1},{1,0},{2,3},{3,2},{4,5},{5,4},{6,7},{7,6},{8,9},{9,8},{10,11... | collective-permute-start | bytes 516104 | tf_op jit(solution)/shard_map/ppermute | solution.py:74
  17.4 64.1 %collective-permute-start.9 = (bf16[24,3584]{1,0:T(8,128)(2,1)}, bf16[24,3584]{1,0:T(8,128)(2,1)S(1)}, u32[]{:S(2)}, u32[]{:S(2)}) collective-permute-start(bf16[24,3584]{1,0:T(8,128)(2,1)} %get-tuple-element.143), channel_id=1, source_target_pairs={{0,2},{1,3},{2,0},{3,1},{4,6},{5,7},{6,4},{7,5},{8,10},{9,11},{10,... | collective-permute-start | bytes 516104 | tf_op jit(solution)/shard_map/ppermute | solution.py:74
  20.0 62.5 %collective-permute-start.10 = (bf16[24,3584]{1,0:T(8,128)(2,1)}, bf16[24,3584]{1,0:T(8,128)(2,1)S(1)}, u32[]{:S(2)}, u32[]{:S(2)}) collective-permute-start(bf16[24,3584]{1,0:T(8,128)(2,1)} %get-tuple-element.143), channel_id=1, source_target_pairs={{0,3},{1,2},{2,1},{3,0},{4,7},{5,6},{6,5},{7,4},{8,11},{9,10},{10,... | collective-permute-start | bytes 516104 | tf_op jit(solution)/shard_map/ppermute | solution.py:74
  22.3 27.6 %collective-permute-start.2 = (bf16[24,1664]{1,0:T(8,128)(2,1)}, bf16[24,1664]{1,0:T(8,128)(2,1)S(1)}, u32[]{:S(2)}, u32[]{:S(2)}) collective-permute-start(bf16[24,1664]{1,0:T(8,128)(2,1)} %get-tuple-element.128), channel_id=1, source_target_pairs={{0,1},{1,0},{2,3},{3,2},{4,5},{5,4},{6,7},{7,6},{8,9},{9,8},{10,11... | collective-permute-start | bytes 239624 | tf_op jit(solution)/shard_map/ppermute | solution.py:74
  23.2 27.6 %collective-permute-start.3 = (bf16[24,1664]{1,0:T(8,128)(2,1)}, bf16[24,1664]{1,0:T(8,128)(2,1)S(1)}, u32[]{:S(2)}, u32[]{:S(2)}) collective-permute-start(bf16[24,1664]{1,0:T(8,128)(2,1)} %get-tuple-element.128), channel_id=1, source_target_pairs={{0,2},{1,3},{2,0},{3,1},{4,6},{5,7},{6,4},{7,5},{8,10},{9,11},{10,... | collective-permute-start | bytes 239624 | tf_op jit(solution)/shard_map/ppermute | solution.py:74
  34.3 56.9 %all-to-all-start = ((bf16[8,24,1536]{2,1,0:T(8,128)(2,1)}), bf16[8,24,1536]{2,1,0:T(8,128)(2,1)S(1)}, u32[]{:S(2)}, u32[]{:S(2)}) async-start(bf16[8,24,1536]{2,1,0:T(8,128)(2,1)} %reshape.858), calls=%async_computation | async-start | bytes 1179648 | tf_op jit(solution)/shard_map/all_to_all | solution.py:241
  71.5 38.7 %collective-permute-start.1 = (bf16[128,768]{1,0:T(8,128)(2,1)}, bf16[128,768]{1,0:T(8,128)(2,1)}, u32[]{:S(2)}, u32[]{:S(2)}) collective-permute-start(bf16[128,768]{1,0:T(8,128)(2,1)} %get-tuple-element.80), channel_id=1, source_target_pairs={{1,0},{2,1},{3,2},{4,3},{5,4},{6,5},{7,6},{8,7},{9,8},{10,9},{11,1... | collective-permute-start | bytes 589832 | tf_op jit(solution)/shard_map/ppermute | solution.py:216
  72.8 39.8 %collective-permute-start = (bf16[128,768]{1,0:T(8,128)(2,1)}, bf16[128,768]{1,0:T(8,128)(2,1)}, u32[]{:S(2)}, u32[]{:S(2)}) collective-permute-start(bf16[128,768]{1,0:T(8,128)(2,1)} %get-tuple-element.79), channel_id=1, source_target_pairs={{0,1},{1,2},{2,3},{3,4},{4,5},{5,6},{6,7},{7,8},{8,9},{9,10},{10,1... | collective-permute-start | bytes 589832 | tf_op jit(solution)/shard_map/ppermute | solution.py:215
  81.5 17.3 %collective-permute-start.17 = (bf16[96,3072]{1,0:T(8,128)(2,1)}, bf16[96,3072]{1,0:T(8,128)(2,1)}, u32[]{:S(2)}, u32[]{:S(2)}) collective-permute-start(bf16[96,3072]{1,0:T(8,128)(2,1)} %pad_maximum_fusion.12), channel_id=1, source_target_pairs={{0,16},{1,17},{2,18},{3,19},{4,12},{5,13},{6,14},{7,15},{8,24},{9,... | collective-permute-start | bytes 1769480 | tf_op jit(solution)/shard_map/ppermute | solution.py:69
  83.6 24.6 %collective-permute-start.11 = (bf16[96,3584]{1,0:T(8,128)(2,1)S(1)}, bf16[96,3584]{1,0:T(8,128)(2,1)S(1)}, u32[]{:S(2)}, u32[]{:S(2)}) collective-permute-start(bf16[96,3584]{1,0:T(8,128)(2,1)S(1)} %pad_maximum_fusion.11), channel_id=1, source_target_pairs={{0,16},{1,17},{2,18},{3,19},{4,12},{5,13},{6,14},{7,15},{8,24},{9,... | collective-permute-start | bytes 2064392 | tf_op jit(solution)/shard_map/ppermute | solution.py:69
  89.7 23.7 %collective-permute-start.6 = (bf16[192,1664]{1,0:T(8,128)(2,1)}, bf16[192,1664]{1,0:T(8,128)(2,1)}, u32[]{:S(2)}, u32[]{:S(2)}) collective-permute-start(bf16[192,1664]{1,0:T(8,128)(2,1)} %get-tuple-element.88), channel_id=1, source_target_pairs={{0,8},{1,9},{2,10},{3,11},{4,20},{5,21},{6,22},{7,23},{8,0},{9,1},... | collective-permute-start | bytes 1916936 | tf_op jit(solution)/shard_map/ppermute | solution.py:69
  98.8 19.1 %collective-permute-start.25 = (bf16[192,1536]{1,0:T(8,128)(2,1)S(1)}, bf16[192,1536]{1,0:T(8,128)(2,1)S(1)}, u32[]{:S(2)}, u32[]{:S(2)}) collective-permute-start(bf16[192,1536]{1,0:T(8,128)(2,1)S(1)} %bitcast.166), channel_id=1, source_target_pairs={{0,3},{1,2},{2,1},{3,0},{4,7},{5,6},{6,5},{7,4},{8,11},{9,10},{10,... | collective-permute-start | bytes 1769480 | tf_op jit(solution)/shard_map/ppermute | solution.py:74
  108.2 38.2 %collective-permute-start.18 = (bf16[192,3072]{1,0:T(8,128)(2,1)}, bf16[192,3072]{1,0:T(8,128)(2,1)}, u32[]{:S(2)}, u32[]{:S(2)}) collective-permute-start(bf16[192,3072]{1,0:T(8,128)(2,1)} %get-tuple-element.75), channel_id=1, source_target_pairs={{0,8},{1,9},{2,10},{3,11},{4,20},{5,21},{6,22},{7,23},{8,0},{9,1},... | collective-permute-start | bytes 3538952 | tf_op jit(solution)/shard_map/ppermute | solution.py:69
  110.1 33.2 %collective-permute-start.24 = (bf16[192,1536]{1,0:T(8,128)(2,1)S(1)}, bf16[192,1536]{1,0:T(8,128)(2,1)}, u32[]{:S(2)}, u32[]{:S(2)}) collective-permute-start(bf16[192,1536]{1,0:T(8,128)(2,1)S(1)} %bitcast.167), channel_id=1, source_target_pairs={{0,2},{1,3},{2,0},{3,1},{4,6},{5,7},{6,4},{7,5},{8,10},{9,11},{10,... | collective-permute-start | bytes 1769480 | tf_op jit(solution)/shard_map/ppermute | solution.py:74
  112.6 30.8 %collective-permute-start.23 = (bf16[192,1536]{1,0:T(8,128)(2,1)S(1)}, bf16[192,1536]{1,0:T(8,128)(2,1)}, u32[]{:S(2)}, u32[]{:S(2)}) collective-permute-start(bf16[192,1536]{1,0:T(8,128)(2,1)S(1)} %bitcast.168), channel_id=1, source_target_pairs={{0,1},{1,0},{2,3},{3,2},{4,5},{5,4},{6,7},{7,6},{8,9},{9,8},{10,11... | collective-permute-start | bytes 1769480 | tf_op jit(solution)/shard_map/ppermute | solution.py:74
  113.5 35.3 %collective-permute-start.12 = (bf16[192,3584]{1,0:T(8,128)(2,1)}, bf16[192,3584]{1,0:T(8,128)(2,1)}, u32[]{:S(2)}, u32[]{:S(2)}) collective-permute-start(bf16[192,3584]{1,0:T(8,128)(2,1)} %get-tuple-element.70), channel_id=1, source_target_pairs={{0,8},{1,9},{2,10},{3,11},{4,20},{5,21},{6,22},{7,23},{8,0},{9,1},... | collective-permute-start | bytes 4128776 | tf_op jit(solution)/shard_map/ppermute | solution.py:69
  118.7 33.1 %collective-permute-start.7 = (bf16[384,1664]{1,0:T(8,128)(2,1)}, bf16[384,1664]{1,0:T(8,128)(2,1)}, u32[]{:S(2)}, u32[]{:S(2)}) collective-permute-start(bf16[384,1664]{1,0:T(8,128)(2,1)} %constant_dynamic-update-slice_fusion.5), channel_id=1, source_target_pairs={{0,4},{1,5},{2,6},{3,7},{4,0},{5,1},{6,2},{7,3},{8,12},{9,13},{10,... | collective-permute-start | bytes 3833864 | tf_op jit(solution)/shard_map/ppermute | solution.py:65
  148.7 27.5 %collective-permute-start.19 = (bf16[384,3072]{1,0:T(8,128)(2,1)}, bf16[384,3072]{1,0:T(8,128)(2,1)}, u32[]{:S(2)}, u32[]{:S(2)}) collective-permute-start(bf16[384,3072]{1,0:T(8,128)(2,1)} %constant_dynamic-update-slice_fusion.40), channel_id=1, source_target_pairs={{0,4},{1,5},{2,6},{3,7},{4,0},{5,1},{6,2},{7,3},{8,12},{9,13},{10,... | collective-permute-start | bytes 7077896 | tf_op jit(solution)/shard_map/ppermute | solution.py:65
  151.3 28.1 %collective-permute-start.13 = (bf16[384,3584]{1,0:T(8,128)(2,1)}, bf16[384,3584]{1,0:T(8,128)(2,1)}, u32[]{:S(2)}, u32[]{:S(2)}) collective-permute-start(bf16[384,3584]{1,0:T(8,128)(2,1)} %constant_dynamic-update-slice_fusion.25), channel_id=1, source_target_pairs={{0,4},{1,5},{2,6},{3,7},{4,0},{5,1},{6,2},{7,3},{8,12},{9,13},{10,... | collective-permute-start | bytes 8257544 | tf_op jit(solution)/shard_map/ppermute | solution.py:65
  224.1 185.8 %collective-permute-start.49 = (bf16[384,3072]{1,0:T(8,128)(2,1)}, bf16[384,3072]{1,0:T(8,128)(2,1)}, u32[]{:S(2)}, u32[]{:S(2)}) collective-permute-start(bf16[384,3072]{1,0:T(8,128)(2,1)} %pad_maximum_fusion.5), channel_id=1, source_target_pairs={{0,4},{1,5},{2,6},{3,7},{4,0},{5,1},{6,2},{7,3},{8,12},{9,13},{10,... | collective-permute-start | bytes 7077896 | tf_op jit(solution)/shard_map/ppermute | solution.py:65
  242.7 18.2 %collective-permute-start.57 = (bf16[192,1536]{1,0:T(8,128)(2,1)S(1)}, bf16[192,1536]{1,0:T(8,128)(2,1)S(1)}, u32[]{:S(2)}, u32[]{:S(2)}) collective-permute-start(bf16[192,1536]{1,0:T(8,128)(2,1)S(1)} %get-tuple-element.54), channel_id=1, source_target_pairs={{0,3},{1,2},{2,1},{3,0},{4,7},{5,6},{6,5},{7,4},{8,11},{9,10},{10,... | collective-permute-start | bytes 1769480 | tf_op jit(solution)/shard_map/ppermute | solution.py:74
  245.3 49.7 %collective-permute-start.56 = (bf16[192,1536]{1,0:T(8,128)(2,1)S(1)}, bf16[192,1536]{1,0:T(8,128)(2,1)S(1)}, u32[]{:S(2)}, u32[]{:S(2)}) collective-permute-start(bf16[192,1536]{1,0:T(8,128)(2,1)S(1)} %get-tuple-element.55), channel_id=1, source_target_pairs={{0,2},{1,3},{2,0},{3,1},{4,6},{5,7},{6,4},{7,5},{8,10},{9,11},{10,... | collective-permute-start | bytes 1769480 | tf_op jit(solution)/shard_map/ppermute | solution.py:74
  245.3 49.7 %collective-permute-start.55 = (bf16[192,1536]{1,0:T(8,128)(2,1)S(1)}, bf16[192,1536]{1,0:T(8,128)(2,1)S(1)}, u32[]{:S(2)}, u32[]{:S(2)}) collective-permute-start(bf16[192,1536]{1,0:T(8,128)(2,1)S(1)} %get-tuple-element.53), channel_id=1, source_target_pairs={{0,1},{1,0},{2,3},{3,2},{4,5},{5,4},{6,7},{7,6},{8,9},{9,8},{10,11... | collective-permute-start | bytes 1769480 | tf_op jit(solution)/shard_map/ppermute | solution.py:74
  253.8 46.6 %collective-permute-start.28 = (bf16[32,1536]{1,0:T(8,128)(2,1)}, bf16[32,1536]{1,0:T(8,128)(2,1)}, u32[]{:S(2)}, u32[]{:S(2)}) collective-permute-start(bf16[32,1536]{1,0:T(8,128)(2,1)} %slice.1047), channel_id=1, source_target_pairs={{0,16},{1,17},{2,18},{3,19},{4,12},{5,13},{6,14},{7,15},{8,24},{9,... | collective-permute-start | bytes 294920 | tf_op jit(solution)/shard_map/ppermute | solution.py:69
  296.1 100.6 %all-to-all-start.1 = ((bf16[8,24,1536]{2,1,0:T(8,128)(2,1)}), bf16[8,24,1536]{2,1,0:T(8,128)(2,1)}, u32[]{:S(2)}, u32[]{:S(2)}) async-start(bf16[8,24,1536]{2,1,0:T(8,128)(2,1)} %bitcast.170), calls=%async_computation.1 | async-start | bytes 1179648 | tf_op jit(solution)/shard_map/all_to_all | solution.py:372
  369.9 19.3 %collective-permute-start.31 = (bf16[512,768]{1,0:T(8,128)(2,1)S(1)}, bf16[512,768]{1,0:T(8,128)(2,1)S(1)}, u32[]{:S(2)}, u32[]{:S(2)}) collective-permute-start(bf16[512,768]{1,0:T(8,128)(2,1)S(1)} %bitcast.188), channel_id=1, source_target_pairs={{0,4},{1,5},{2,6},{3,7},{4,0},{5,1},{6,2},{7,3},{8,12},{9,13},{10,... | collective-permute-start | bytes 2359304 | tf_op jit(solution)/shard_map/ppermute | solution.py:65
  379.4 36.7 %collective-permute-start.30 = (bf16[128,768]{1,0:T(8,128)(2,1)}, bf16[128,768]{1,0:T(8,128)(2,1)}, u32[]{:S(2)}, u32[]{:S(2)}) collective-permute-start(bf16[128,768]{1,0:T(8,128)(2,1)} %get-tuple-element.78), channel_id=1, source_target_pairs={{1,0},{2,1},{3,2},{4,3},{5,4},{6,5},{7,6},{8,7},{9,8},{10,9},{11,1... | collective-permute-start | bytes 589832 | tf_op jit(solution)/shard_map/ppermute | solution.py:463
  380.7 35.4 %collective-permute-start.29 = (bf16[128,768]{1,0:T(8,128)(2,1)}, bf16[128,768]{1,0:T(8,128)(2,1)}, u32[]{:S(2)}, u32[]{:S(2)}) collective-permute-start(bf16[128,768]{1,0:T(8,128)(2,1)} %get-tuple-element.77), channel_id=1, source_target_pairs={{0,1},{1,2},{2,3},{3,4},{4,5},{5,6},{6,7},{7,8},{8,9},{9,10},{10,1... | collective-permute-start | bytes 589832 | tf_op jit(solution)/shard_map/ppermute | solution.py:464
  415.4 39.4 %collective-permute-start.43 = (bf16[384,3584]{1,0:T(8,128)(2,1)}, bf16[384,3584]{1,0:T(8,128)(2,1)}, u32[]{:S(2)}, u32[]{:S(2)}) collective-permute-start(bf16[384,3584]{1,0:T(8,128)(2,1)} %pad_maximum_fusion.3), channel_id=1, source_target_pairs={{0,4},{1,5},{2,6},{3,7},{4,0},{5,1},{6,2},{7,3},{8,12},{9,13},{10,... | collective-permute-start | bytes 8257544 | tf_op jit(solution)/shard_map/ppermute | solution.py:65
  435.7 21.8 %collective-permute-start.38 = (bf16[192,1664]{1,0:T(8,128)(2,1)S(1)}, bf16[192,1664]{1,0:T(8,128)(2,1)S(1)}, u32[]{:S(2)}, u32[]{:S(2)}) collective-permute-start(bf16[192,1664]{1,0:T(8,128)(2,1)S(1)} %slice.1041), channel_id=1, source_target_pairs={{0,8},{1,9},{2,10},{3,11},{4,20},{5,21},{6,22},{7,23},{8,0},{9,1},... | collective-permute-start | bytes 1916936 | tf_op jit(solution)/shard_map/ppermute | solution.py:69
  457.1 18.4 %collective-permute-start.44 = (bf16[192,3584]{1,0:T(8,128)(2,1)S(1)}, bf16[192,3584]{1,0:T(8,128)(2,1)S(1)}, u32[]{:S(2)}, u32[]{:S(2)}) collective-permute-start(bf16[192,3584]{1,0:T(8,128)(2,1)S(1)} %slice.1038), channel_id=1, source_target_pairs={{0,8},{1,9},{2,10},{3,11},{4,20},{5,21},{6,22},{7,23},{8,0},{9,1},... | collective-permute-start | bytes 4128776 | tf_op jit(solution)/shard_map/ppermute | solution.py:69
  (173 other events, 1379.6 us)
Sparse Core Ops, SparseCore 0:
  29.4 58.6 all-gather.1
where the time goes:
time: 517 us; the launch traced here: 510 us
  waiting for transfers between devices  148 us (29%)
  matrix products  147 us (28%)
  starting transfers between devices  81.5 us (16%)
  local copies, waits for them, and re-layouts  71.5 us (14%)
  other arithmetic  44.2 us (9%)
  between operations  17.9 us (3%)
    dot_general x73, matrix products, dot(): lax.dot_general(left, right, (dims, ((), ())), preferred_element_type=F32)  113 us
    ppermute x27, waiting for transfers between devices, by_z(): return lax.ppermute(array, AXES, self.pairs(lambda p, c, z: (p, c, z ^ k)))  89 us
    ppermute x18, waiting for transfers between devices, by_bit(): lax.ppermute(array, AXES, self.pairs(lambda p, c, z: (p ^ 1 << (j if c el...  58.8 us
    ppermute x27, starting transfers between devices, by_z(): return lax.ppermute(array, AXES, self.pairs(lambda p, c, z: (p, c, z ^ k)))  39.1 us
    unnamed x309, local copies, waits for them, and re-layouts  29.1 us
    dot_general x11, matrix products, per_head(): return jnp.einsum(pattern, left, right, preferred_element_type=F32)  21.4 us
    ppermute x18, starting transfers between devices, by_bit(): lax.ppermute(array, AXES, self.pairs(lambda p, c, z: (p ^ 1 << (j if c el...  18.7 us
    concatenate x6, local copies, waits for them, and re-layouts, gather_seq(): shard = jnp.concatenate([shard, self.by_bit(shard, j)], axis=0)  11.6 us
  transfers between devices with their start and end apart: 61, of which 18 were waited for; matrix products, arithmetic and copies ran while one was open for 40% of the time, Pallas kernels for 0%

commit v1 on v0

v1 whole, which is shorter than its diff:
```python
import functools
import math

import jax
import jax.numpy as jnp
from jax import lax
from jax.experimental import pallas as pl
from jax.experimental.pallas import tpu as pltpu
from jax.sharding import PartitionSpec as P

HL = 8
HDL = 64
HH = 12
HDH = 64
RADIUS = 128

NEG = -1e30
EPS = 1e-06
HIGH = lax.Precision.HIGHEST
AXES = ("seq", "fsdp")
F32 = jnp.float32
BF16 = jnp.bfloat16
ROOM = 12 << 20
PACE = 1e9
TIMES = {
    "pack": 2.5,
    "select": 3.2,
    "prepare": 0.8,
    "light_rows": 1.8,
    "light_forward": 4.2,
    "heavy_rows": 8.7,
    "heavy_forward": 2.7,
    "join": 2.1,
    "feed": 4.4,
    "feed_weight": 1.4,
    "expert": 6.0,
    "turn": 2.9,
    "heavy_scores": 4.0,
    "heavy_weights": 10.0,
    "light_scores": 5.6,
    "light_weights": 3.4,
    "finish": 2.9,
}


def dot(left, right, dims):
    return lax.dot_general(left, right, (dims, ((), ())), preferred_element_type=F32)


def nn(left, right):
    return dot(left, right, ((1,), (0,)))


def nt(left, right):
    return dot(left, right, ((1,), (1,)))


def tn(left, right):
    return dot(left, right, ((0,), (0,)))


def reverse_bits(value, count):
    out = value * 0
    for j in range(count):
        out = out | (((value >> j) & 1) << (count - 1 - j))
    return out


class Net:
    def __init__(self):
        self.seq = lax.axis_size("seq")
        self.depth = lax.axis_size("fsdp")
        self.levels = (self.seq // 2).bit_length() - 1
        self.count = self.seq * self.depth
        s = lax.axis_index("seq")
        self.core, self.pair = s & 1, s >> 1
        self.z = lax.axis_index("fsdp")
        self.device = s * self.depth + self.z

    def pairs(self, move):
        out = []
        for s in range(self.seq):
            for z in range(self.depth):
                pair, core, to_z = move(s >> 1, s & 1, z)
                out.append((s * self.depth + z, (pair * 2 + core) * self.depth + to_z))
        return out

    def by_core(self, array):
        return lax.ppermute(array, AXES, self.pairs(lambda p, c, z: (p, 1 - c, z)))

    def by_bit(self, array, j):
        top = self.levels - 1 - j
        return lax.ppermute(
            array, AXES, self.pairs(lambda p, c, z: (p ^ (1 << (j if c else top)), c, z))
        )

    def by_z(self, array, k):
        return lax.ppermute(array, AXES, self.pairs(lambda p, c, z: (p, c, z ^ k)))

    def target(self, relative):
        zr = relative % self.depth
        bits = (relative // self.depth) % (self.seq // 2)
        core = self.core ^ (relative // (self.count // 2))
        pair = self.pair ^ jnp.where(core == 1, bits, reverse_bits(bits, self.levels))
        return (pair * 2 + core) * self.depth + (self.z ^ zr)

    def from_z(self, shard):
        return [shard] + [self.by_z(shard, k) for k in range(1, self.depth)]

    def exchange_z(self, pieces):
        return [pieces[0]] + [self.by_z(pieces[k], k) for k in range(1, self.depth)]

    def gather(self, shard):
        shard = jnp.concatenate(self.from_z(shard), axis=0)
        for j in range(self.levels):
            shard = jnp.concatenate([shard, self.by_bit(shard, j)], axis=0)
        return shard, self.by_core(shard)

    def reduce(self, keep, send):
        keep, send = fold(keep, self.by_core(send), 2)
        for j in reversed(range(self.levels)):
            pieces = 2 if j else self.depth
            out = fold(keep, self.by_bit(send, j), pieces)
            keep, send = out[0], out[1]
        return self.exchange_z(out)

    def members(self):
        relative = jnp.arange(2 * self.depth, dtype=jnp.int32)
        core = self.core ^ (relative // self.depth)
        return core * self.depth + (self.z ^ (relative % self.depth))


class Order:
    def __init__(self):
        self.last = ()

    def hold(self, array):
        return after(array, *self.last)

    def note(self, array):
        self.last = (array,)
        return array


def stack_rows(arrays):
    height = sum(a.shape[0] for a in arrays)
    if len(arrays) < 3 or any(a.shape[0] % 8 for a in arrays):
        return jnp.concatenate(arrays, axis=0)

    def body(*refs):
        at = 0
        for ref in refs[:-1]:
            refs[-1][at : at + ref.shape[0]] = ref[...]
            at += ref.shape[0]

    return run(body, "stack", [((height, arrays[0].shape[1]), arrays[0].dtype)], arrays)[0]


def after(array, *earlier):
    return lax.optimization_barrier((array, *earlier))[0]


def unit_rms(values):
    scale = lax.rsqrt(jnp.mean(values * values, -1, keepdims=True) + EPS)
    return values * scale, scale


def norm_back(grad, gain, unit, scale):
    scaled = grad * gain
    return scale * (scaled - unit * jnp.mean(scaled * unit, -1, keepdims=True))


def document_of(places, lengths):
    return (places >= lengths[0]).astype(jnp.int32)


def sigmoid(values):
    return 1.0 / (1.0 + jnp.exp(-values))


def soft(scores):
    top = jnp.max(scores, -1, keepdims=True)
    expo = jnp.exp(scores - top)
    return expo / jnp.sum(expo, -1, keepdims=True)


def two_parts(values):
    high = values.astype(BF16)
    return high, (values - high.astype(F32)).astype(BF16)


def place_rows(select, values):
    high, low = two_parts(values)
    return tn(select, high) + tn(select, low)


def take_rows(select, values):
    high, low = two_parts(values)
    return nn(select, high) + nn(select, low)


def reorder(values, order):
    high, low = two_parts(values)
    return nn(high, order) + nn(low, order)


def reorder_back(values, order):
    high, low = two_parts(values)
    return nt(high, order) + nt(low, order)


def into(values, first, second):
    half = first.shape[0]
    return nn(values[:, :half], first) + nn(values[:, half:], second)


def onto(values, first, second):
    return jnp.concatenate([nt(values, first), nt(values, second)], axis=1)


def lanes(rows, width=128):
    return lax.broadcasted_iota(jnp.int32, (rows, width), 1)


def both_heads(pair):
    first = lanes(pair.shape[0]) < HDL
    zero = jnp.zeros_like(pair)
    return jnp.concatenate([jnp.where(first, pair, zero), jnp.where(first, zero, pair)], axis=0)


def one_pair(stacked):
    rows = stacked.shape[0] // 2
    return jnp.where(lanes(rows) < HDL, stacked[:rows], stacked[rows:])


def run(body, name, outs, args, smem=0, scratch=(), columns=None, room=ROOM):
    vmem = pl.BlockSpec(memory_space=pltpu.VMEM)
    specs = [pl.BlockSpec(memory_space=pltpu.SMEM)] * smem + [vmem] * (len(args) - smem)
    for i, count in (columns or {}).items():
        specs[i] = pl.BlockSpec(
            (args[i].shape[0], count), lambda i: (0, 0), pipeline_mode=pl.Buffered(1)
        )
    held = sum(math.prod(piece.shape) * jnp.dtype(piece.dtype).itemsize for piece in scratch)
    return pl.pallas_call(
        body,
        name=name,
        compiler_params=pltpu.CompilerParams(vmem_limit_bytes=held + room),
        out_shape=[jax.ShapeDtypeStruct(shape, kind) for shape, kind in outs],
        grid=(1,) if columns else (),
        in_specs=specs,
        out_specs=[vmem] * len(outs),
        scratch_shapes=list(scratch),
        cost_estimate=pl.CostEstimate(flops=int(TIMES.get(name, 1.0) * PACE) + 1, bytes_accessed=1, transcendentals=0),
    )(*args)


def fold(keep, moved, pieces, kind=BF16):
    height, width = keep.shape
    piece = height // pieces
    parts = 2 if piece % 32 == 0 else 1
    step = piece // parts

    def body(*refs):
        for k in range(pieces):
            total = refs[k][...].astype(F32) + refs[pieces + k][...].astype(F32)
            refs[2 * pieces + k][...] = total.astype(kind)

    def spec(k):
        return pl.BlockSpec((step, width), lambda i, k=k: (k * parts + i, 0))

    if piece % 8:
        total = keep.astype(F32) + moved.astype(F32)
        return [total[k * piece : (k + 1) * piece].astype(kind) for k in range(pieces)]
    return pl.pallas_call(
        body,
        name="fold",
        compiler_params=pltpu.CompilerParams(vmem_limit_bytes=ROOM),
        grid=(parts,),
        out_shape=[jax.ShapeDtypeStruct((piece, width), kind)] * pieces,
        in_specs=[spec(k) for k in range(pieces)] * 2,
        out_specs=[spec(0)] * pieces,
        cost_estimate=pl.CostEstimate(flops=int(0.6 * PACE) + 1, bytes_accessed=1, transcendentals=0),
    )(*([keep] * pieces + [moved] * pieces))


def settle(pieces, widths, name):
    def body(*refs):
        parts, outs = refs[: len(pieces)], refs[len(pieces) :]
        at = 0
        for out, width in zip(outs, widths):
            total = parts[0][:, at : at + width].astype(F32)
            for part in parts[1:]:
                total = total + part[:, at : at + width].astype(F32)
            out[...] = total
            at += width

    rows = pieces[0].shape[0]
    return run(body, name, [((rows, width), F32) for width in widths], pieces)


def hot(column, rows):
    return jnp.where(column == lanes(column.shape[0], rows), 1.0, 0.0).astype(BF16)


def as_column(row):
    count = row.shape[1]
    eye = lax.broadcasted_iota(jnp.int32, (count, count), 0) == lanes(count, count)
    spread = jnp.where(eye, row.astype(F32), 0.0)
    return jnp.sum(spread, -1, keepdims=True).astype(jnp.int32)


def order_matrix(order):
    width = order.shape[1]
    rows = lax.broadcasted_iota(jnp.int32, (width, width), 0)
    return jnp.where(rows == order, 1.0, 0.0).astype(BF16)


def select_body(
    place, orders, query_route, key_route, feed_route, cotangent, to_own, to_slice, cot, query_select, key_select, feed_select, query_doc
):
    rows = cotangent.shape[0]
    to_own[...] = order_matrix(orders[0:1])
    to_slice[...] = order_matrix(orders[1:2])
    cot[...] = nn(cotangent[...], to_own[...]).astype(BF16)
    queries = as_column(query_route[pl.ds(place[4], 1)])
    query_select[...] = hot(queries, rows)
    key_select[...] = hot(as_column(key_route[pl.ds(place[4], 1)]), rows)
    feed_select[...] = hot(as_column(feed_route[...]), rows)
    query_doc[...] = jnp.where(place[0] + queries >= place[1], 1, 0)


def pack_body(
    place, key_spots, tokens, key_route, q_l, k_l, v_l, o_l, o_s, gate_s, up_s, down_s, gate_l, up_l, down_l,
    second, third, expert_keep, expert_send, key_docs
):
    part, width = q_l.shape
    at = 0
    for ref in (o_l, o_s, q_l, k_l, v_l):
        second[:, at : at + ref.shape[1]] = ref[...]
        at += ref.shape[1]
    keyed = nn(hot(as_column(key_route[pl.ds(place[4], 1)]), tokens.shape[0]), tokens[...])
    second[:, at : at + width] = keyed[:part].astype(BF16)
    rest = keyed[part:]
    chunk = width * rest.shape[0] // part
    pieces = [rest[:, i * chunk : (i + 1) * chunk] for i in range(width // chunk)]
    second[:, at + width :] = jnp.concatenate(pieces, axis=0).astype(BF16)
    narrow = gate_s.shape[1]
    for i, ref in enumerate((gate_s, up_s, down_s)):
        third[:, i * narrow : (i + 1) * narrow] = ref[...]
    share = expert_keep.shape[1] // 3
    depth = expert_keep.shape[0] // part
    for c, expert in enumerate((expert_keep, expert_send)):
        for k in range(depth):
            at = ((place[5] ^ c) * depth + (place[6] ^ k)) * share
            at = pl.ds(pl.multiple_of(at, share), share)
            for i, ref in enumerate((gate_l, up_l, down_l)):
                expert[k * part : (k + 1) * part, i * share : (i + 1) * share] = ref[:, at]
    blocks, slots = key_route.shape
    keys = key_spots.shape[1]
    block = lax.broadcasted_iota(jnp.int32, (blocks, keys), 0) == key_spots[0:1]
    table = key_route[...].astype(F32).T.astype(BF16)
    found = nn(table, jnp.where(block, 1.0, 0.0).astype(BF16))
    slot = lax.broadcasted_iota(jnp.int32, (slots, keys), 0) == key_spots[1:2]
    position = jnp.sum(jnp.where(slot, found, 0.0), 0, keepdims=True).astype(jnp.int32)
    rows = tokens.shape[0]
    document = jnp.where(key_spots[0:1] * rows + position >= place[1], 1, 0)
    key_docs[...] = jnp.where(position < rows, document, -1)


def prepare_body(to_own, above, tokens, below, raw):
    order = to_own[...]
    at = 0
    for ref in (above, tokens, below):
        raw[at : at + ref.shape[0]] = nn(ref[...], order).astype(BF16)
        at += ref.shape[0]


def unpack_body(place, keep, got, gate, up, down):
    part = gate.shape[0]
    depth = keep.shape[0] // part
    share = keep.shape[1] // 3
    for c, source in enumerate((keep, got)):
        for k in range(depth):
            at = ((place[5] ^ c) * depth + (place[6] ^ k)) * share
            at = pl.ds(pl.multiple_of(at, share), share)
            for i, out in enumerate((gate, up, down)):
                piece = source[k * part : (k + 1) * part, i * share : (i + 1) * share]
                out[:, at] = piece.astype(F32)


def pair_up(first, second, part):
    count = first.shape[0] // part
    width = first.shape[1]
    if part % 8:
        cuts = [slice(k * part, (k + 1) * part) for k in range(count)]
        return [jnp.concatenate([first[c], second[c]], axis=0) for c in cuts]

    def body(*refs):
        for k in range(count):
            for i in range(2):
                refs[2 + k][i * part : (i + 1) * part] = refs[i][k * part : (k + 1) * part]

    return run(body, "pair_up", [((2 * part, width), BF16)] * count, (first, second))


def take_apart(pieces, part):
    width = pieces[0].shape[1]
    count = len(pieces)
    if part % 8:
        return [jnp.concatenate([p[i * part : (i + 1) * part] for p in pieces], axis=0) for i in range(2)]

    def body(*refs):
        for k in range(count):
            for i in range(2):
                refs[count + i][k * part : (k + 1) * part] = refs[k][i * part : (i + 1) * part]

    return run(body, "take_apart", [((count * part, width), BF16)] * 2, pieces)


def local_mask(place, tile, reach, stacked, span):
    shape = (stacked, span)
    row = lax.broadcasted_iota(jnp.int32, shape, 0) & (reach - 1)
    query = place[0] + tile * reach + row
    key = place[0] + (tile - 1) * reach + lax.broadcasted_iota(jnp.int32, shape, 1)
    split, live, total = place[1], place[1] + place[2], place[3]
    inside = (key >= 0) & (key < total)
    same = jnp.where(query >= split, 1, 0) == jnp.where(key >= split, 1, 0)
    near = jnp.abs(query - key) <= reach
    both = ((query < live) & (key < live)) | (query == key)
    return near & inside & same & both


def light_rows_body(raw, w0, w1, normed, queries, pairs, vectors):
    light = HL * HDL
    reach = RADIUS
    rows = queries.shape[0]
    columns = [w[:, 3 * light :].astype(F32).T[:8] for w in (w0, w1)]
    vectors[...] = jnp.concatenate(columns, axis=1)
    unit, unused = unit_rms(raw[...].astype(F32))
    normed[...] = (unit * vectors[0:1]).astype(BF16)
    own = normed[reach : reach + rows]
    queries[...] = into(own, w0[:, :light], w1[:, :light]).astype(BF16)
    pairs[...] = into(normed[...], w0[:, light : 3 * light], w1[:, light : 3 * light]).astype(BF16)


def light_forward_body(place, queries, pairs, mixed, sums):
    light = HL * HDL
    reach = RADIUS
    rows = queries.shape[0]
    scale = 1.0 / math.sqrt(HDL)
    lane = lanes(reach)
    for tile in range(rows // reach):
        mine = slice(tile * reach, (tile + 1) * reach)
        seen = slice(tile * reach, (tile + 3) * reach)
        mask = local_mask(place, tile, reach, 2 * reach, 3 * reach)
        logs = jnp.zeros((reach, 128), F32)
        for p in range(HL // 2):
            at = slice(p * 128, (p + 1) * 128)
            query = both_heads(queries[mine, at])
            scores = jnp.where(mask, nt(query, pairs[seen, at]) * scale, NEG)
            top = jnp.max(scores, -1, keepdims=True)
            expo = jnp.exp(scores - top)
            total = jnp.sum(expo, -1, keepdims=True)
            probs = (expo * (1.0 / total)).astype(BF16)
            value = pairs[seen, light + p * 128 : light + (p + 1) * 128]
            mixed[mine, at] = one_pair(nn(probs, value)).astype(BF16)
            log = top + jnp.log(total)
            logs = jnp.where(lane == 2 * p, log[:reach], logs)
            logs = jnp.where(lane == 2 * p + 1, log[reach:], logs)
        sums[mine] = logs


def piece_select(block_rows, rest, part, piece):
    shape = (block_rows // part * rest, block_rows)
    k = lax.broadcasted_iota(jnp.int32, shape, 0)
    row = lax.broadcasted_iota(jnp.int32, shape, 1)
    shift = rest.bit_length() - 1
    want = (k >> shift) * part + piece * rest + (k & (rest - 1))
    return jnp.where(row == want, 1.0, 0.0).astype(BF16)


def heavy_rows_body(select, normed, vectors, to_own, s0, s1, keyed, pairs, routed, queries, held):
    width = normed.shape[1]
    heavy = HH * HDH
    half = s0.shape[0]
    slots = routed.shape[0]
    at = width + HL * HDL + 3 * heavy
    q_at = slice(width + HL * HDL, width + HL * HDL + heavy)
    kv_at = slice(width + HL * HDL + heavy, at)
    part = half // (keyed.shape[0] // slots // 2)
    rest = slots - part
    chunk = width * rest // part
    for i, ref in enumerate((s0, s1)):
        held[i * half : (i + 1) * half] = ref[:, at : at + width]
        low = 2 * half + i * (half // part * rest)
        for piece in range(part // rest):
            picked = nn(piece_select(half, rest, part, piece), ref[:, at + width :])
            held[low : low + half // part * rest, piece * chunk : (piece + 1) * chunk] = picked.astype(BF16)
    step = 256

    def project(t, carry):
        rows = pl.ds(pl.multiple_of(t * step, step), step)
        unit, unused = unit_rms(nn(held[rows], to_own[...]))
        keyed[rows] = (unit * vectors[0:1]).astype(BF16)
        pairs[rows] = into(keyed[rows], s0[:, kv_at], s1[:, kv_at]).astype(BF16)
        return carry

    lax.fori_loop(0, keyed.shape[0] // step, project, 0)
    own = normed[RADIUS : normed.shape[0] - RADIUS]
    routed[...] = nn(select[...], own).astype(BF16)
    queries[...] = into(routed[...], s0[:, q_at], s1[:, q_at]).astype(BF16)


def heavy_forward_body(query_doc, key_doc, queries, pairs, mixed, sums):
    heavy = HH * HDH
    slots = queries.shape[0]
    scale = 1.0 / math.sqrt(HDH)
    mask = jnp.concatenate([query_doc[...], query_doc[...]], axis=0) == key_doc[...]
    logs = jnp.zeros((2 * slots, 128), F32)
    for p in range(HH // 2):
        at = slice(p * 128, (p + 1) * 128)
        scores = jnp.where(mask, nt(both_heads(queries[:, at]), pairs[:, at]) * scale, NEG)
        top = jnp.max(scores, -1, keepdims=True)
        expo = jnp.exp(scores - top)
        total = jnp.sum(expo, -1, keepdims=True)
        probs = (expo * (1.0 / total)).astype(BF16)
        mixed[:, at] = one_pair(nn(probs, pairs[:, heavy + p * 128 : heavy + (p + 1) * 128])).astype(BF16)
        logs = jnp.where(lanes(2 * slots) == p, top + jnp.log(total), logs)
    sums[...] = logs


def join_body(
    raw, light_mixed, heavy_mixed, routed, query_select, feed_select, vectors, cot, to_own, s0, s1,
    middle, normed, heavy_branch, feed_rows, feed_grads, sent
):
    heavy = HH * HDH
    width = raw.shape[1]
    rows = middle.shape[0]
    at = slice(heavy, heavy + HL * HDL)
    light_branch = onto(light_mixed[...], s0[:, at], s1[:, at])
    at = slice(0, heavy)
    heavy_branch[...] = onto(heavy_mixed[...], s0[:, at], s1[:, at])
    score = sigmoid(jnp.sum(routed[...].astype(F32) * vectors[1:2], -1, keepdims=True))
    inputs = raw[RADIUS : RADIUS + rows].astype(F32)
    middle[...] = inputs + light_branch + place_rows(query_select[...], score * heavy_branch[...])
    unit, unused = unit_rms(middle[...])
    normed[...] = (unit * vectors[2:3]).astype(BF16)
    feed_rows[...] = nn(feed_select[...], normed[...]).astype(BF16)
    feed_grads[...] = nn(feed_select[...], cot[...])
    score = sigmoid(jnp.sum(feed_rows[...].astype(F32) * vectors[3:4], -1, keepdims=True))
    sent[:, :width] = nt(feed_rows[...], to_own[...]).astype(BF16)
    sent[:, width:] = nt((score * feed_grads[...]).astype(BF16), to_own[...]).astype(BF16)


def geglu_rows(gate, upper, grad_hidden):
    c0, c1 = 0.7978845608028654, 0.044715
    square = gate * gate
    bent = jnp.tanh(c0 * gate * (1.0 + c1 * square))
    bell = 0.5 * (1.0 + bent)
    gelu = gate * bell
    slope = bell + 0.5 * gate * (1.0 - bent * bent) * (c0 * (1.0 + 3.0 * c1 * square))
    return gelu * upper, grad_hidden * upper * slope, grad_hidden * gelu


def geglu_loop(wide, grad_hidden, hidden, grads):
    count = hidden.shape[1]
    step = 32

    def rows_at(t, carry):
        rows = pl.ds(pl.multiple_of(t * step, step), step)
        out, grad_gate, grad_upper = geglu_rows(
            wide[rows, :count], wide[rows, count:], grad_hidden[rows]
        )
        hidden[rows] = out.astype(BF16)
        grads[rows, :count] = grad_gate.astype(BF16)
        grads[rows, count:] = grad_upper.astype(BF16)
        return carry

    lax.fori_loop(0, hidden.shape[0] // step, rows_at, 0)


def feed_body(normed, cot, t0, t1, feed, grad_normed, hidden, grads, wide, grad_hidden):
    narrow = hidden.shape[1]
    wide[...] = into(normed[...], t0[:, : 2 * narrow], t1[:, : 2 * narrow])
    grad_hidden[...] = into(cot[...], t0[:, 2 * narrow :], t1[:, 2 * narrow :])
    geglu_loop(wide, grad_hidden, hidden, grads)
    feed[...] = onto(hidden[...], t0[:, 2 * narrow :], t1[:, 2 * narrow :])
    grad_normed[...] = onto(grads[...], t0[:, : 2 * narrow], t1[:, : 2 * narrow])


def feed_weight_body(normed, cot, hidden, grads, keep, send):
    narrow = hidden.shape[1]
    half = keep.shape[0]
    for out, at in ((send, slice(half, None)), (keep, slice(0, half))):
        out[:, : 2 * narrow] = tn(normed[:, at], grads[...]).astype(out.dtype)
        out[:, 2 * narrow :] = tn(cot[:, at], hidden[...]).astype(out.dtype)


def expert_body(got0, got1, to_slice, weights, keep, send, grad_keep, grad_send, rows, row_grads, wide, grad_hidden, hidden, grads):
    width = to_slice.shape[0]
    share = hidden.shape[1]
    count = got0.shape[0]
    for i, got in enumerate((got0, got1)):
        at = slice(i * count, (i + 1) * count)
        rows[at] = nn(got[:, :width], to_slice[...]).astype(BF16)
        row_grads[at] = nn(got[:, width:], to_slice[...]).astype(BF16)
    wide[...] = nn(rows[...], weights[:, : 2 * share])
    grad_hidden[...] = nn(row_grads[...], weights[:, 2 * share :])
    geglu_loop(wide, grad_hidden, hidden, grads)
    for out, at in ((send, slice(count, None)), (keep, slice(0, count))):
        feed = nt(hidden[at], weights[:, 2 * share :]).astype(BF16)
        back = nt(grads[at], weights[:, : 2 * share]).astype(BF16)
        out[:, :width] = nt(feed, to_slice[...]).astype(out.dtype)
        out[:, width:] = nt(back, to_slice[...]).astype(out.dtype)
    half = grad_keep.shape[0]
    for out, at in ((grad_send, slice(half, None)), (grad_keep, slice(0, half))):
        out[:, : 2 * share] = tn(rows[:, at], grads[...]).astype(out.dtype)
        out[:, 2 * share :] = tn(row_grads[:, at], hidden[...]).astype(out.dtype)


def turn_body(*refs):
    pieces = refs[:-12]
    (
        middle, feed, grad_normed, feed_rows, feed_grads, feed_select, vectors, cot, to_own,
        result, grad_middle, vector_grads,
    ) = refs[-12:]
    width = middle.shape[1]
    summed = pieces[0][...].astype(F32)
    for piece in pieces[1:]:
        summed = summed + piece[...].astype(F32)
    feed_heavy = reorder(summed[:, :width], to_own[...])
    grad_rows = reorder(summed[:, width:], to_own[...])
    rows = feed_rows[...].astype(F32)
    score = sigmoid(jnp.sum(rows * vectors[3:4], -1, keepdims=True))
    logit = jnp.sum(feed_grads[...] * feed_heavy, -1, keepdims=True) * score * (1.0 - score)
    grad_rows = grad_rows + logit * vectors[3:4]
    grads = grad_normed[...] + place_rows(feed_select[...], grad_rows)
    unit, scale = unit_rms(middle[...])
    grad_middle[...] = cot[...].astype(F32) + norm_back(grads, vectors[2:3], unit, scale)
    vector_grads[...] = jnp.concatenate(
        [
            jnp.zeros((2, width), F32),
            jnp.sum(grads * unit, 0, keepdims=True),
            jnp.sum(rows * logit, 0, keepdims=True),
            jnp.zeros((4, width), F32),
        ],
        axis=0,
    )
    out = middle[...] + feed[...] + place_rows(feed_select[...], score * feed_heavy)
    result[...] = nt(out.astype(BF16), to_own[...]).astype(BF16)


def heavy_scores_body(
    query_doc, key_doc, grad_middle, query_select, routed, pairs, queries, heavy_branch, sums, vectors, s0, s1,
    grad_branch, grad_queries, grad_pairs, logits
):
    heavy = HH * HDH
    score = sigmoid(jnp.sum(routed[...].astype(F32) * vectors[1:2], -1, keepdims=True))
    grad_rows = take_rows(query_select[...], grad_middle[...])
    grad_branch[...] = (score * grad_rows).astype(BF16)
    logit = jnp.sum(grad_rows * heavy_branch[...], -1, keepdims=True) * score * (1.0 - score)
    logits[...] = jnp.broadcast_to(logit, logits.shape)
    at = slice(0, heavy)
    grad_mixed = into(grad_branch[...], s0[:, at], s1[:, at]).astype(BF16)
    scale = 1.0 / math.sqrt(HDH)
    mask = jnp.concatenate([query_doc[...], query_doc[...]], axis=0) == key_doc[...]
    for p in range(HH // 2):
        at = slice(p * 128, (p + 1) * 128)
        beyond = slice(heavy + p * 128, heavy + (p + 1) * 128)
        query = both_heads(queries[:, at])
        grad_out = both_heads(grad_mixed[:, at])
        scores = jnp.where(mask, nt(query, pairs[:, at]) * scale, NEG)
        probs = jnp.exp(scores - sums[:, p : p + 1])
        grad_probs = nt(grad_out, pairs[:, beyond])
        delta = jnp.sum(probs * grad_probs, -1, keepdims=True)
        grad_scores = (probs * (grad_probs - delta)).astype(BF16)
        grad_queries[:, at] = one_pair(nn(grad_scores, pairs[:, at]) * scale).astype(BF16)
        grad_pairs[:, at] = (tn(grad_scores, query) * scale).astype(BF16)
        grad_pairs[:, beyond] = tn(probs.astype(BF16), grad_out).astype(BF16)


def heavy_weights_body(
    grad_middle, routed, keyed, light_mixed, heavy_mixed, grad_branch, grad_queries, grad_pairs, logits, vectors, to_own, s0, s1,
    keep, send, grad_routed, vector_grads, moved
):
    width = grad_middle.shape[1]
    heavy = HH * HDH
    light = HL * HDL
    half = s0.shape[0]
    slots = routed.shape[0]
    q_at = slice(width + light, width + light + heavy)
    kv_at = slice(width + light + heavy, width + light + 3 * heavy)
    logit = logits[:, 0:1]
    grad_routed[...] = onto(grad_queries[...], s0[:, q_at], s1[:, q_at]) + logit * vectors[1:2]
    step = 256

    def back(t, gain):
        rows = pl.ds(pl.multiple_of(t * step, step), step)
        grads = onto(grad_pairs[rows], s0[:, kv_at], s1[:, kv_at])
        moved[rows] = nt(grads.astype(BF16), to_own[...]).astype(BF16)
        return gain + jnp.sum(grads * keyed[rows].astype(F32), 0, keepdims=True)

    gain = lax.fori_loop(0, keyed.shape[0] // step, back, jnp.zeros((1, width), F32))
    vector_grads[...] = jnp.concatenate(
        [
            gain / vectors[0:1],
            jnp.sum(routed[...].astype(F32) * logit, 0, keepdims=True),
            jnp.zeros((6, width), F32),
        ],
        axis=0,
    )
    low = grad_middle[...].astype(BF16)
    part = half // (keyed.shape[0] // slots // 2)
    rest = slots - part
    chunk = width * rest // part
    for i, out in ((1, send), (0, keep)):
        at = slice(i * half, (i + 1) * half)
        out[:, :width] = tn(grad_branch[:, at], heavy_mixed[...]).astype(BF16)
        out[:, width : width + light] = tn(low[:, at], light_mixed[...]).astype(BF16)
        out[:, q_at] = tn(routed[:, at], grad_queries[...]).astype(BF16)
        out[:, kv_at] = tn(keyed[:, at], grad_pairs[...]).astype(BF16)
        to = width + light + 3 * heavy
        out[:, to : to + width] = moved[at]
        at = 2 * half + i * (half // part * rest)
        total = 0.0
        for piece in range(part // rest):
            block = moved[at : at + half // part * rest, piece * chunk : (piece + 1) * chunk]
            total = total + tn(piece_select(half, rest, part, piece), block)
        out[:, to + width :] = total.astype(BF16)


def light_scores_body(place, grad_middle, queries, pairs, sums, s0, s1, grad_queries, grad_pairs, held):
    light = HL * HDL
    heavy = HH * HDH
    reach = RADIUS
    rows = queries.shape[0]
    at = slice(heavy, heavy + light)
    grad_mixed = into(grad_middle[...].astype(BF16), s0[:, at], s1[:, at]).astype(BF16)
    held[...] = jnp.zeros_like(held)
    scale = 1.0 / math.sqrt(HDL)
    for tile in range(rows // reach):
        mine = slice(tile * reach, (tile + 1) * reach)
        seen = slice(tile * reach, (tile + 3) * reach)
        mask = local_mask(place, tile, reach, 2 * reach, 3 * reach)
        for p in range(HL // 2):
            at = slice(p * 128, (p + 1) * 128)
            beyond = slice(light + p * 128, light + (p + 1) * 128)
            query = both_heads(queries[mine, at])
            grad_out = both_heads(grad_mixed[mine, at])
            key = pairs[seen, at]
            log = jnp.concatenate([sums[mine, 2 * p : 2 * p + 1], sums[mine, 2 * p + 1 : 2 * p + 2]], axis=0)
            probs = jnp.exp(jnp.where(mask, nt(query, key) * scale, NEG) - log)
            grad_probs = nt(grad_out, pairs[seen, beyond])
            delta = jnp.sum(probs * grad_probs, -1, keepdims=True)
            grad_scores = (probs * (grad_probs - delta)).astype(BF16)
            grad_queries[mine, at] = one_pair(nn(grad_scores, key) * scale).astype(BF16)
            held[seen, at] = held[seen, at] + tn(grad_scores, query) * scale
            held[seen, beyond] = held[seen, beyond] + tn(probs.astype(BF16), grad_out)
    grad_pairs[...] = held[...].astype(BF16)


def light_weights_body(
    raw, normed, grad_queries, grad_pairs, grad_routed, query_select, feed_vectors, heavy_vectors, to_own, f0, f1,
    keep, send, outer, grad_mine
):
    light = HL * HDL
    reach = RADIUS
    rows = grad_queries.shape[0]
    half = f0.shape[0]
    grads = onto(grad_pairs[...], f0[:, light : 3 * light], f1[:, light : 3 * light])
    for i, at in enumerate((slice(0, reach), slice(reach + rows, None))):
        outer[i * reach : (i + 1) * reach] = nt(grads[at].astype(BF16), to_own[...]).astype(BF16)
    own = onto(grad_queries[...], f0[:, :light], f1[:, :light])
    own = own + grads[reach : reach + rows] + place_rows(query_select[...], grad_routed[...])
    grad_mine[...] = own
    unit, unused = unit_rms(raw[...].astype(F32))
    gain = jnp.sum(own * unit[reach : reach + rows], 0, keepdims=True)
    for at in (slice(0, reach), slice(reach + rows, None)):
        gain = gain + jnp.sum(grads[at] * unit[at], 0, keepdims=True)
    vector_rows = feed_vectors[...] + heavy_vectors[...]
    first = lax.broadcasted_iota(jnp.int32, vector_rows.shape, 0) == 0
    vector_rows = vector_rows + jnp.where(first, gain, 0.0)
    filler = jnp.zeros((120, raw.shape[1]), F32)
    columns = jnp.concatenate([vector_rows, filler], axis=0)
    for i, out in ((1, send), (0, keep)):
        at = slice(i * half, (i + 1) * half)
        out[:, :light] = tn(normed[reach : reach + rows, at], grad_queries[...]).astype(BF16)
        out[:, light : 3 * light] = tn(normed[:, at], grad_pairs[...]).astype(BF16)
        out[:, 3 * light :] = columns[:, at].T.astype(BF16)


def finish_body(from_prev, from_next, keyed_grads, key_select, grad_mine, grad_middle, raw, vectors, to_own, out):
    reach = RADIUS
    rows, width = grad_mine.shape
    order = to_own[...]
    grads = [grad_mine[:reach] + nn(from_prev[...], order)]
    if rows > 2 * reach:
        grads.append(grad_mine[reach : rows - reach])
    grads.append(grad_mine[rows - reach :] + nn(from_next[...], order))
    keyed = keyed_grads[...]
    if keyed.shape[0] < key_select.shape[0]:
        rest = key_select.shape[0] - keyed.shape[0]
        tail = [keyed[i * rest : (i + 1) * rest, width:] for i in range(keyed.shape[0] // rest)]
        keyed = jnp.concatenate([keyed[:, :width], jnp.concatenate(tail, axis=1)], axis=0)
    keyed = nn(keyed.astype(BF16), order).astype(BF16)
    total = jnp.concatenate(grads, axis=0) + tn(key_select[...], keyed)
    unit, scale = unit_rms(raw[reach : reach + rows].astype(F32))
    total = grad_middle[...] + norm_back(total, vectors[0:1], unit, scale)
    out[...] = reorder_back(total, order)


def heavy_forward_wide(query_doc, key_doc, select, normed, vectors, to_own, s0, s1, keyed_raw):
    heavy = HH * HDH
    at = vectors.shape[1] + HL * HDL
    q_at, kv_at = slice(at, at + heavy), slice(at + heavy, at + 3 * heavy)
    unit, unused = unit_rms(nn(keyed_raw, to_own))
    keyed = (unit * vectors[0:1]).astype(BF16)
    pairs = into(keyed, s0[:, kv_at], s1[:, kv_at]).astype(BF16)
    routed = nn(select, normed[RADIUS : normed.shape[0] - RADIUS]).astype(BF16)
    queries = into(routed, s0[:, q_at], s1[:, q_at]).astype(BF16)

    def heads(array):
        return array.reshape(-1, HH, HDH)

    scores = jnp.einsum(
        "qhd,khd->hqk", heads(queries), heads(pairs[:, :heavy]), preferred_element_type=F32
    ) / math.sqrt(HDH)
    probs = soft(jnp.where((query_doc == key_doc)[None], scores, NEG))
    mixed = jnp.einsum(
        "hqk,khd->qhd", probs.astype(BF16), heads(pairs[:, heavy:]), preferred_element_type=F32
    )
    return keyed, pairs, routed, queries, mixed.reshape(-1, heavy).astype(BF16), probs


def heavy_backward_wide(
    grad_middle, query_select, routed, keyed, pairs, queries, light_mixed, heavy_mixed, heavy_branch, probs,
    vectors, to_own, s0, s1
):
    heavy = HH * HDH
    scale = 1.0 / math.sqrt(HDH)
    half = s0.shape[0]
    at = vectors.shape[1] + HL * HDL
    q_at, kv_at = slice(at, at + heavy), slice(at + heavy, at + 3 * heavy)
    score = sigmoid(jnp.sum(routed.astype(F32) * vectors[1:2], -1, keepdims=True))
    grad_rows = take_rows(query_select, grad_middle)
    grad_branch = (score * grad_rows).astype(BF16)
    logit = jnp.sum(grad_rows * heavy_branch, -1, keepdims=True) * score * (1.0 - score)
    at = slice(0, heavy)
    grad_mixed = into(grad_branch, s0[:, at], s1[:, at]).astype(BF16)

    def heads(array):
        return array.reshape(-1, HH, HDH)

    def mix(pattern, left, right):
        return jnp.einsum(pattern, left, right, preferred_element_type=F32)

    grad_probs = mix("qhd,khd->hqk", heads(grad_mixed), heads(pairs[:, heavy:]))
    delta = jnp.sum(probs * grad_probs, -1, keepdims=True)
    grad_scores = (probs * (grad_probs - delta)).astype(BF16)
    grad_queries = mix("hqk,khd->qhd", grad_scores, heads(pairs[:, :heavy])) * scale
    grad_queries = grad_queries.reshape(-1, heavy).astype(BF16)
    grad_keys = mix("hqk,qhd->khd", grad_scores, heads(queries)) * scale
    grad_values = mix("hqk,qhd->khd", probs.astype(BF16), heads(grad_mixed))
    grad_pairs = jnp.concatenate(
        [grad_keys.reshape(-1, heavy).astype(BF16), grad_values.reshape(-1, heavy).astype(BF16)], axis=1
    )
    grad_routed = onto(grad_queries, s0[:, q_at], s1[:, q_at]) + logit * vectors[1:2]
    grads = onto(grad_pairs, s0[:, kv_at], s1[:, kv_at])
    vector_grads = jnp.concatenate(
        [
            jnp.sum(grads * keyed.astype(F32), 0, keepdims=True) / vectors[0:1],
            jnp.sum(routed.astype(F32) * logit, 0, keepdims=True),
            jnp.zeros((6, grads.shape[1]), F32),
        ],
        axis=0,
    )
    moved = nt(grads.astype(BF16), to_own).astype(BF16)
    low = grad_middle.astype(BF16)
    sides = []
    for at in (slice(0, half), slice(half, None)):
        columns = (
            tn(grad_branch[:, at], heavy_mixed),
            tn(low[:, at], light_mixed),
            tn(routed[:, at], grad_queries),
            tn(keyed[:, at], grad_pairs),
        )
        sides.append(jnp.concatenate(columns, axis=1).astype(BF16))
    return sides[0], sides[1], grad_routed, vector_grads, moved


def per_device(
    tokens,
    query_small,
    key_small,
    value_small,
    out_small,
    query_large,
    key_large,
    value_large,
    out_large,
    attend_gain,
    attend_router,
    gate_small,
    up_small,
    down_small,
    gate_large,
    up_large,
    down_large,
    feed_gain,
    feed_router,
    lengths,
    query_route,
    key_route,
    feed_route,
    cotangent,
):
    net = Net()
    rows, width = tokens.shape
    blocks = net.count
    part = width // blocks
    half = width // 2
    first = net.device * rows
    light = HL * HDL
    heavy = HH * HDH
    narrow = down_small.shape[0]
    wide = down_large.shape[0]
    slots = query_route.shape[1]
    members = 2 * net.depth
    share = wide // members
    pooled = members * slots
    keys = blocks * slots
    rest = slots - part
    packed = part % 8 == 0 and rest > 0 and rest % 8 == 0 and part % rest == 0 and keys <= 2048

    step = [(i, i + 1) for i in range(blocks - 1)]
    back = [(i + 1, i) for i in range(blocks - 1)]
    vector_pack = jnp.stack([attend_gain, attend_router, feed_gain, feed_router], axis=1)
    vector_pack = jnp.pad(vector_pack, ((0, 0), (0, 124)))
    first_parts = net.from_z(
        jnp.concatenate([query_small, key_small, value_small, vector_pack], axis=1)
    )
    above = lax.ppermute(tokens[rows - RADIUS :], AXES, step)
    below = lax.ppermute(tokens[:RADIUS], AXES, back)
    column = jnp.arange(width, dtype=jnp.int32)
    own_order = net.target(column // part) * part + column % part
    bits = column // part // members
    bits = jnp.where(net.core == 1, bits, reverse_bits(bits, net.levels))
    member = column // part % members
    member = (net.core ^ (member % 2)) * net.depth + (net.z ^ (member // 2))
    slice_order = ((net.pair ^ bits) * members + member) * part + column % part
    orders = jnp.stack([own_order, slice_order])
    place = jnp.stack([first, lengths[0], lengths[1], jnp.int32(rows * blocks), net.device, net.core, net.z])
    square = ((width, width), BF16)
    chosen = ((slots, rows), BF16)

    if packed:
        tall = blocks * part
        spot = jnp.arange(keys, dtype=jnp.int32)
        spot_block = jnp.where(spot < tall, spot // part, (spot - tall) // rest)
        spot_slot = jnp.where(spot < tall, spot % part, part + (spot - tall) % rest)
        second_set, third_set, slices_keep, slices_send, key_docs = run(
            pack_body,
            "pack",
            [
                ((part, 5 * width + light + width * rest // part), BF16),
                ((part, 3 * narrow), BF16),
                ((net.depth * part, 3 * share), BF16),
                ((net.depth * part, 3 * share), BF16),
                ((1, keys), jnp.int32),
            ],
            (
                place, jnp.stack([net.target(spot_block), spot_slot]), tokens, key_route,
                query_large, key_large, value_large, out_large.T, out_small.T,
                gate_small, up_small, down_small.T, gate_large, up_large, down_large.T,
            ),
            smem=1,
            room=56 << 20,
        )
    else:
        second_set = jnp.concatenate(
            [out_large.T, out_small.T, query_large, key_large, value_large], axis=1
        )
        third_set = jnp.concatenate([gate_small, up_small, down_small.T], axis=1)
        stacked = jnp.stack([gate_large, up_large, down_large.T], axis=0)
        stacked = stacked.reshape(3, part, members, share).transpose(2, 1, 0, 3)
        stacked = jnp.take(stacked.reshape(members, part, 3 * share), net.members(), axis=0)
        slices_keep, slices_send = stacked.reshape(2, net.depth * part, 3 * share)
    order = Order()
    top_bit = net.levels - 1

    def take_z(pieces):
        return order.note(stack_rows([order.hold(pieces[0])] + pieces[1:]))

    def take(whole, moved):
        return order.note(jnp.concatenate([whole, order.hold(moved)], axis=0))

    def first_moved(whole):
        return net.by_bit(whole, 0)

    def rest_moved(whole, moved):
        for j in range(1, net.levels):
            whole = take(whole, moved)
            moved = net.by_bit(whole, j)
        return whole, moved

    order.note(second_set)
    first_set = take_z(first_parts)
    first_moving = first_moved(first_set)
    second_parts = net.from_z(after(second_set, first_set))
    to_own, to_slice, cot, query_select, key_select, feed_select, query_docs = run(
        select_body,
        "select",
        [square, square, ((rows, width), BF16), chosen, chosen, chosen, ((slots, 1), jnp.int32)],
        (place, orders, query_route, key_route, feed_route, order.hold(cotangent)),
        smem=1,
        room=56 << 20,
    )
    order.note(cot)
    first_set, first_moving = rest_moved(first_set, first_moving)
    second_set = take_z(second_parts)
    (raw,) = run(
        prepare_body,
        "prepare",
        [((rows + 2 * RADIUS, width), BF16)],
        (order.hold(to_own), above, tokens, below),
    )
    order.note(raw)
    f0 = take(first_set, first_moving)
    f1 = net.by_core(f0)
    second_moving = first_moved(after(second_set, f0))
    third_parts = net.from_z(after(third_set, second_set))

    normed_ext, query_rows, pair_rows, vectors = run(
        light_rows_body,
        "light_rows",
        [
            ((rows + 2 * RADIUS, width), BF16),
            ((rows, light), BF16),
            ((rows + 2 * RADIUS, 2 * light), BF16),
            ((8, width), F32),
        ],
        (order.hold(raw), f0, f1),
    )
    order.note(query_rows)
    second_set, second_moving = rest_moved(second_set, second_moving)
    slices_got = net.by_core(after(slices_send, query_rows))
    light_mixed, light_sums = run(
        light_forward_body,
        "light_forward",
        [((rows, light), BF16), ((rows, 128), F32)],
        (place, order.hold(query_rows), pair_rows),
        smem=1,
    )
    order.note(light_mixed)
    third_set = take_z(third_parts)
    slices = net.exchange_z(pair_up(after(slices_keep, third_set), slices_got, part))
    s0 = take(second_set, second_moving)
    s1 = net.by_core(s0)
    third_moving = first_moved(after(third_set, s0))
    expert = take_z(slices)

    if packed:
        keyed, heavy_pairs, routed, routed_query = run(
            heavy_rows_body,
            "heavy_rows",
            [
                ((keys, width), BF16),
                ((keys, 2 * heavy), BF16),
                ((slots, width), BF16),
                ((slots, heavy), BF16),
            ],
            (order.hold(query_select), normed_ext, vectors, to_own, s0, s1),
            scratch=[pltpu.VMEM((keys, width), BF16)],
        )
        order.note(routed_query)
        third_set, third_moving = rest_moved(third_set, third_moving)
        heavy_mixed, heavy_sums = run(
            heavy_forward_body,
            "heavy_forward",
            [((slots, heavy), BF16), ((2 * slots, 128), F32)],
            (query_docs, key_docs, order.hold(routed_query), heavy_pairs),
        )
    else:
        relative = net.target(jnp.arange(blocks, dtype=jnp.int32))
        near_routes = jnp.take(key_route, relative, axis=0)
        key_docs = document_of(relative[:, None] * rows + near_routes, lengths)
        key_docs = jnp.where(near_routes < rows, key_docs, -1).reshape(1, -1)
        keyed_raw = net.gather(nn(key_select, tokens).astype(BF16))
        keyed, heavy_pairs, routed, routed_query, heavy_mixed, heavy_sums = heavy_forward_wide(
            query_docs, key_docs, query_select, normed_ext, vectors, to_own, s0, s1,
            jnp.concatenate(keyed_raw, axis=0),
        )
        third_set, third_moving = rest_moved(third_set, third_moving)
    order.note(heavy_mixed)

    middle, normed_two, heavy_branch, feed_rows, feed_grads, sent = run(
        join_body,
        "join",
        [
            ((rows, width), F32),
            ((rows, width), BF16),
            ((slots, width), F32),
            ((slots, width), BF16),
            ((slots, width), F32),
            ((slots, 2 * width), BF16),
        ],
        (
            raw, light_mixed, order.hold(heavy_mixed), routed, query_select, feed_select, vectors, cot, to_own, s0, s1,
        ),
        columns={9: heavy + light, 10: heavy + light},
    )
    order.note(sent)

    got_parts = net.from_z(sent)
    t0 = take(third_set, third_moving)
    t1 = net.by_core(t0)
    expert_moving = first_moved(after(expert, t0))
    got0 = take_z(got_parts)
    got1 = net.by_core(got0)
    feed_light, grad_normed, hidden, hidden_grads = run(
        feed_body,
        "feed",
        [
            ((rows, width), F32),
            ((rows, width), F32),
            ((rows, narrow), BF16),
            ((rows, 2 * narrow), BF16),
        ],
        (order.hold(normed_two), cot, t0, t1),
        scratch=[pltpu.VMEM((rows, 2 * narrow), F32), pltpu.VMEM((rows, narrow), F32)],
    )
    order.note(hidden)
    expert, expert_moving = rest_moved(expert, expert_moving)
    third_keep, third_send = run(
        feed_weight_body,
        "feed_weight",
        [((half, 3 * narrow), BF16), ((half, 3 * narrow), BF16)],
        (normed_two, cot, order.hold(hidden), hidden_grads),
    )
    order.note(third_send)
    third_moving = net.by_core(third_send)
    expert = take(expert, expert_moving)
    keep, send, expert_keep, expert_send = run(
        expert_body,
        "expert",
        [
            ((pooled // 2, 2 * width), BF16),
            ((pooled // 2, 2 * width), BF16),
            ((half, 3 * share), BF16),
            ((half, 3 * share), BF16),
        ],
        (order.hold(got0), got1, to_slice, expert),
        scratch=[
            pltpu.VMEM((pooled, width), BF16),
            pltpu.VMEM((pooled, width), BF16),
            pltpu.VMEM((pooled, 2 * share), F32),
            pltpu.VMEM((pooled, share), F32),
            pltpu.VMEM((pooled, share), BF16),
            pltpu.VMEM((pooled, 2 * share), BF16),
        ],
    )
    order.note(send)
    moving = net.by_core(send)
    expert_moving = net.by_bit(expert_send, top_bit)

    def give(keep, moved, pieces):
        out = fold(keep, order.hold(moved), pieces)
        order.note(out[0])
        return out

    def descend(keep, moved):
        for j in reversed(range(net.levels - 1)):
            keep, send = give(keep, moved, 2)
            moved = net.by_bit(send, j)
        return keep, moved

    third_keep, third_send = give(third_keep, third_moving, 2)
    summed = net.exchange_z(give(keep, moving, net.depth))
    third_moving = net.by_bit(third_send, top_bit)

    result, grad_middle, feed_vectors = run(
        turn_body,
        "turn",
        [((rows, width), BF16), ((rows, width), F32), ((8, width), F32)],
        (
            order.hold(summed[0]), *summed[1:], middle, feed_light, grad_normed, feed_rows, feed_grads, feed_select,
            vectors, cot, to_own,
        ),
    )
    order.note(grad_middle)
    expert_keep, expert_moving = descend(expert_keep, expert_moving)
    if packed:
        grad_branch, grad_queries, grad_heavy_pairs, logits = run(
            heavy_scores_body,
            "heavy_scores",
            [
                ((slots, width), BF16),
                ((slots, heavy), BF16),
                ((keys, 2 * heavy), BF16),
                ((slots, 128), F32),
            ],
            (
                query_docs, key_docs, order.hold(grad_middle), query_select, routed, heavy_pairs, routed_query,
                heavy_branch, heavy_sums, vectors, s0, s1,
            ),
            columns={10: heavy + light, 11: heavy + light},
        )
        order.note(grad_branch)
    expert_parts = net.exchange_z(give(expert_keep, expert_moving, net.depth))
    third_keep, third_moving = descend(third_keep, third_moving)
    if packed:
        second_keep, second_send, grad_routed, heavy_vectors = run(
            heavy_weights_body,
            "heavy_weights",
            [
                ((half, 5 * width + light + width * rest // part), BF16),
                ((half, 5 * width + light + width * rest // part), BF16),
                ((slots, width), F32),
                ((8, width), F32),
            ],
            (
                grad_middle, routed, keyed, light_mixed, heavy_mixed, order.hold(grad_branch), grad_queries,
                grad_heavy_pairs, logits, vectors, to_own, s0, s1,
            ),
            scratch=[pltpu.VMEM((keys, width), BF16)],
            columns={11: 4 * heavy + light, 12: 4 * heavy + light},
        )
    else:
        second_keep, second_send, grad_routed, heavy_vectors, keyed_grads = heavy_backward_wide(
            grad_middle, query_select, routed, keyed, heavy_pairs, routed_query, light_mixed, heavy_mixed,
            heavy_branch, heavy_sums, vectors, to_own, s0, s1,
        )
    order.note(second_send)
    second_moving = net.by_core(second_send)
    expert_keep, expert_send = take_apart([order.hold(expert_parts[0])] + expert_parts[1:], part)
    order.note(expert_send)
    expert_got = net.by_core(expert_send)
    third_parts = net.exchange_z(give(third_keep, third_moving, net.depth))
    grad_queries, grad_pairs = run(
        light_scores_body,
        "light_scores",
        [((rows, light), BF16), ((rows + 2 * RADIUS, 2 * light), BF16)],
        (place, order.hold(grad_middle), query_rows, pair_rows, light_sums, s0, s1),
        smem=1,
        scratch=[pltpu.VMEM((rows + 2 * RADIUS, 2 * light), F32)],
        columns={5: heavy + light, 6: heavy + light},
    )
    order.note(grad_queries)
    second_keep, second_send = give(second_keep, second_moving, 2)
    second_moving = net.by_bit(second_send, top_bit)
    first_keep, first_send, outer, grad_mine = run(
        light_weights_body,
        "light_weights",
        [
            ((half, 3 * light + 128), BF16),
            ((half, 3 * light + 128), BF16),
            ((2 * RADIUS, width), BF16),
            ((rows, width), F32),
        ],
        (
            raw, normed_ext, order.hold(grad_queries), grad_pairs, grad_routed, query_select, feed_vectors, heavy_vectors,
            to_own, f0, f1,
        ),
    )
    order.note(first_send)
    first_moving = net.by_core(first_send)
    from_next = lax.ppermute(outer[:RADIUS], AXES, back)
    from_prev = lax.ppermute(outer[RADIUS:], AXES, step)

    if packed:
        gate_grad, up_grad, down_grad = run(
            unpack_body,
            "unpack",
            [((part, wide), F32)] * 3,
            (place, order.hold(expert_keep), expert_got),
            smem=1,
        )
    else:
        expert_grad = jnp.concatenate([order.hold(expert_keep), expert_got], axis=0)
        expert_grad = jnp.take(expert_grad.reshape(members, part, 3 * share), net.members(), axis=0)
        expert_grad = expert_grad.reshape(members, part, 3, share).transpose(2, 1, 0, 3)
        gate_grad, up_grad, down_grad = expert_grad.reshape(3, part, wide).astype(F32)
    order.note(gate_grad)
    first_keep, first_send = give(first_keep, first_moving, 2)
    first_moving = net.by_bit(first_send, top_bit)
    third_grad = settle([order.hold(third_parts[0])] + third_parts[1:], [narrow] * 3, "settle_third")
    order.note(third_grad[0])
    second_keep, second_moving = descend(second_keep, second_moving)
    first_keep, first_moving = descend(first_keep, first_moving)
    second_parts = net.exchange_z(give(second_keep, second_moving, net.depth))
    first_parts = net.exchange_z(give(first_keep, first_moving, net.depth))
    widths = [width, light, heavy, heavy, heavy]
    if packed:
        widths.append(width + width * rest // part)
    second_grad = settle([order.hold(second_parts[0])] + second_parts[1:], widths, "settle_second")
    order.note(second_grad[0])
    if packed:
        keyed_own = second_grad[5]
    else:
        cut = keys // 2
        keyed_own = settle(net.reduce(keyed_grads[:cut], keyed_grads[cut:]), [width], "settle_keyed")[0]
    first_grad = settle(
        [order.hold(first_parts[0])] + first_parts[1:], [light, light, light, 128], "settle_first"
    )
    order.note(first_grad[0])
    (tokens_grad,) = run(
        finish_body,
        "finish",
        [((rows, width), F32)],
        (
            from_prev, from_next, keyed_own, key_select, grad_mine, grad_middle, raw, vectors, to_own,
        ),
    )
    vector_out = first_grad[3][:, :4].T
    return (
        result,
        tokens_grad,
        first_grad[0],
        first_grad[1],
        first_grad[2],
        second_grad[1].T,
        second_grad[2],
        second_grad[3],
        second_grad[4],
        second_grad[0].T,
        vector_out[0],
        vector_out[1],
        third_grad[0],
        third_grad[1],
        third_grad[2].T,
        gate_grad,
        up_grad,
        down_grad.T,
        vector_out[2],
        vector_out[3],
    )


def solution(mesh):
    by_rows = P(AXES, None)
    by_columns = P(None, AXES)
    vector = P(AXES)
    return jax.shard_map(
        per_device,
        mesh=mesh,
        in_specs=(
            by_rows,
            by_rows,
            by_rows,
            by_rows,
            by_columns,
            by_rows,
            by_rows,
            by_rows,
            by_columns,
            vector,
            vector,
            by_rows,
            by_rows,
            by_columns,
            by_rows,
            by_rows,
            by_columns,
            vector,
            vector,
            P(),
            P(),
            P(),
            by_rows,
            by_rows,
        ),
        out_specs=(
            by_rows,
            by_rows,
            by_rows,
            by_rows,
            by_rows,
            by_columns,
            by_rows,
            by_rows,
            by_rows,
            by_columns,
            vector,
            vector,
            by_rows,
            by_rows,
            by_columns,
            by_rows,
            by_rows,
            by_columns,
            vector,
            vector,
        ),
        check_vma=False,
    )
```

time: 517 us -> 335 us (0.65)
  matrix products: 147 us -> 0 us
  Pallas kernels: 0 us -> 74.5 us
  local copies, waits for them, and re-layouts: 71.5 us -> 2.21 us
  other arithmetic: 44.2 us -> 4.07 us
  between operations: 17.9 us -> 1.44 us
  waiting for transfers between devices: 148 us -> 162 us
    dot_general x90 -> x0, matrix products: 143 us -> none  [the longest x73 113 us: dot(): lax.dot_general(left, right, (dims, ((), ())), preferred_element_type=F32)]
    pallas_call x0 -> x40, Pallas kernels: none -> 74.5 us  [the longest x28 70.7 us: run(): pl.pallas_call(body, name=name, compiler_params=pltpu.CompilerParams(vmem...]
    unnamed x309 -> x28, local copies, waits for them, and re-layouts: 29.1 us -> 0.08 us
    slice x40 -> x2, local copies, waits for them, and re-layouts: 15.3 us -> 0.05 us  [the longest x1 0.03 us: per_device(): from_next = lax.ppermute(outer[:RADIUS], AXES, back)]
    concatenate x6 -> x0, local copies, waits for them, and re-layouts: 11.6 us -> none  [gather_seq(): shard = jnp.concatenate([shard, self.by_bit(shard, j)], axis=0)]
    add x20 -> x1, other arithmetic: 11.4 us -> 0.12 us  [per_device(): slice_order = ((net.pair ^ bits) * members + member) * part + column % part]
    concatenate x12 -> x9, other arithmetic: 11.3 us -> 1.94 us  [the longest x8 1.16 us: take(): return order.note(jnp.concatenate([whole, order.hold(moved)], axis=0))]
    ppermute x9 -> x10, waiting for transfers between devices: 0.02 us -> 9.12 us  [by_core(): return lax.ppermute(array, AXES, self.pairs(lambda p, c, z: (p, 1 - c, z)))]
  transfers between devices with their start and end apart: 61 -> 60, of which waited for: 18 -> 30; matrix products, arithmetic and copies ran while one was open for 40% -> 1% of each run, Pallas kernels for 0% -> 18%
where the time goes in v1:
time: 335 us; the launch traced here: 329 us
  waiting for transfers between devices  162 us (48%)
  starting transfers between devices  84.9 us (25%)
  Pallas kernels  74.5 us (22%)
  other arithmetic  4.07 us (1%)
    ppermute x30, waiting for transfers between devices, by_z(): return lax.ppermute(array, AXES, self.pairs(lambda p, c, z: (p, c, z ^ k)))  86.1 us
    pallas_call x28, Pallas kernels, run(): pl.pallas_call(body, name=name, compiler_params=pltpu.CompilerParams(vmem...  70.7 us
    ppermute x16, waiting for transfers between devices, by_bit(): lax.ppermute(array, AXES, self.pairs(lambda p, c, z: (p ^ 1 << (j if c el...  66.7 us
    ppermute x30, starting transfers between devices, by_z(): return lax.ppermute(array, AXES, self.pairs(lambda p, c, z: (p, c, z ^ k)))  46 us
    ppermute x16, starting transfers between devices, by_bit(): lax.ppermute(array, AXES, self.pairs(lambda p, c, z: (p ^ 1 << (j if c el...  19.8 us
    ppermute x1, starting transfers between devices, per_device(): above = lax.ppermute(tokens[rows - RADIUS:], AXES, step)  9.98 us
    ppermute x10, waiting for transfers between devices, by_core(): return lax.ppermute(array, AXES, self.pairs(lambda p, c, z: (p, 1 - c, z)))  9.12 us
  transfers between devices with their start and end apart: 60, of which 30 were waited for; matrix products, arithmetic and copies ran while one was open for 1% of the time, Pallas kernels for 18%

profile of v1, /device:TPU:0, one launch (start us, length us, event | category | flops | bytes accessed | tf_op | source)
XLA Modules:
  0.0 329.1 jit_solution(54064821867676176)
XLA Ops:
  2.3 5.1 %collective-permute-start.2 = (bf16[24,1664]{1,0:T(8,128)(2,1)S(1)}, bf16[24,1664]{1,0:T(8,128)(2,1)S(1)}, u32[]{:S(2)}, u32[]{:S(2)}) collective-permute-start(bf16[24,1664]{1,0:T(8,128)(2,1)S(1)} %fusion.1.refs_0_), channel_id=1, source_target_pairs={{0,3},{1,2},{2,1},{3,0},{4,7},{5,6},{6,5},{7,4},{8,11},{9,10},{10,... | collective-permute-start | bytes 239624 | tf_op jit(solution)/shard_map/ppermute | solution.py:98
  16.3 3.2 select.235
  28.5 4.5 %collective-permute-done.6.refs_3_ = bf16[24,4608]{1,0:T(8,128)(2,1)S(1)} collective-permute-done((bf16[24,4608]{1,0:T(8,128)(2,1)S(1)}, bf16[24,4608]{1,0:T(8,128)(2,1)S(1)}, u32[]{:S(2)}, u32[]{:S(2)}) %collective-permute-start.6) | collective-permute-done | bytes 221216 | tf_op jit(solution)/shard_map/ppermute | solution.py:98
  32.9 10.0 %collective-permute-start.7 = (bf16[128,768]{1,0:T(8,128)(2,1)S(1)}, bf16[128,768]{1,0:T(8,128)(2,1)S(1)}, u32[]{:S(2)}, u32[]{:S(2)}) collective-permute-start(bf16[128,768]{1,0:T(8,128)(2,1)S(1)} %get-tuple-element.355), channel_id=1, source_target_pairs={{0,1},{1,2},{2,3},{3,4},{4,5},{5,6},{6,7},{7,8},{8,9},{9,10},{10,1... | collective-permute-start | bytes 589832 | tf_op jit(solution)/shard_map/ppermute | solution.py:942
  42.9 5.7 %collective-permute-done.5.refs_2_ = bf16[24,4608]{1,0:T(8,128)(2,1)S(1)} collective-permute-done((bf16[24,4608]{1,0:T(8,128)(2,1)S(1)}, bf16[24,4608]{1,0:T(8,128)(2,1)S(1)}, u32[]{:S(2)}, u32[]{:S(2)}) %collective-permute-start.5) | collective-permute-done | bytes 221216 | tf_op jit(solution)/shard_map/ppermute | solution.py:98
  54.4 8.3 %collective-permute-done.11 = bf16[96,4608]{1,0:T(8,128)(2,1)S(1)} collective-permute-done((bf16[96,4608]{1,0:T(8,128)(2,1)S(1)}, bf16[96,4608]{1,0:T(8,128)(2,1)S(1)}, u32[]{:S(2)}, u32[]{:S(2)}) %collective-permute-start.11) | collective-permute-done | bytes 884768 | tf_op jit(solution)/shard_map/ppermute | solution.py:93
  68.9 4.2 %light_forward.1 = (bf16[256,512]{1,0:T(8,128)(2,1)S(1)}, f32[256,128]{1,0:T(8,128)S(1)}) custom-call(s32[7]{0:T(128)S(1)} %copy-done.5, bf16[256,512]{1,0:T(8,128)(2,1)S(1)} %get-tuple-element.198.queries, bf16[512,1024]{1,0:T(8,128)(2,1)S(1)} %get-tuple-element.199.pairs), custom_call_target="tpu_custom_call" | custom-call | flops 4200000000 | bytes 1 | tf_op jit(solution)/shard_map/light_forward/pallas_call | solution.py:244
  73.1 6.8 %collective-permute-done.13.refs_2_ = bf16[24,3072]{1,0:T(8,128)(2,1)S(1)} collective-permute-done((bf16[24,3072]{1,0:T(8,128)(2,1)S(1)}, bf16[24,3072]{1,0:T(8,128)(2,1)S(1)}, u32[]{:S(2)}, u32[]{:S(2)}) %collective-permute-start.13) | collective-permute-done | bytes 147488 | tf_op jit(solution)/shard_map/ppermute | solution.py:98
  80.0 5.5 %collective-permute-done.16 = bf16[192,4608]{1,0:T(8,128)(2,1)S(1)} collective-permute-done((bf16[192,4608]{1,0:T(8,128)(2,1)S(1)}, bf16[192,4608]{1,0:T(8,128)(2,1)S(1)}, u32[]{:S(2)}, u32[]{:S(2)}) %collective-permute-start.16) | collective-permute-done | bytes 1769504 | tf_op jit(solution)/shard_map/ppermute | solution.py:93
  86.5 6.1 %collective-permute-done.15.refs_1_ = bf16[96,1536]{1,0:T(8,128)(2,1)S(1)} collective-permute-done((bf16[96,1536]{1,0:T(8,128)(2,1)S(1)}, bf16[96,1536]{1,0:T(8,128)(2,1)S(1)}, u32[]{:S(2)}, u32[]{:S(2)}) %collective-permute-start.15) | collective-permute-done | bytes 294944 | tf_op jit(solution)/shard_map/ppermute | solution.py:89
  97.8 3.5 %collective-permute-done.17.refs_1_ = bf16[48,1536]{1,0:T(8,128)(2,1)S(1)} collective-permute-done((bf16[48,1536]{1,0:T(8,128)(2,1)S(1)}, bf16[48,1536]{1,0:T(8,128)(2,1)S(1)}, u32[]{:S(2)}, u32[]{:S(2)}) %collective-permute-start.17) | collective-permute-done | bytes 147488 | tf_op jit(solution)/shard_map/ppermute | solution.py:98
  101.3 8.0 %collective-permute-done.18.refs_2_ = bf16[48,1536]{1,0:T(8,128)(2,1)S(1)} collective-permute-done((bf16[48,1536]{1,0:T(8,128)(2,1)S(1)}, bf16[48,1536]{1,0:T(8,128)(2,1)S(1)}, u32[]{:S(2)}, u32[]{:S(2)}) %collective-permute-start.18) | collective-permute-done | bytes 147488 | tf_op jit(solution)/shard_map/ppermute | solution.py:98
  110.0 8.8 %heavy_rows.1 = (bf16[1024,768]{1,0:T(8,128)(2,1)S(1)}, bf16[1024,1536]{1,0:T(8,128)(2,1)S(1)}, bf16[32,768]{1,0:T(8,128)(2,1)S(1)}, bf16[32,768]{1,0:T(8,128)(2,1)S(1)}) custom-call(bf16[32,256]{1,0:T(8,128)(2,1)S(1)} %copy-done.3, bf16[512,768]{1,0:T(8,128)(2,1)S(1)} %get-tuple-element.218.normed, f32[8,768]{1,0:T(8,128)S(1)} %get-tuple-element.219.vectors.refs_10_, ...), custom_call_target="tpu_custom_call" | custom-call | flops 8700000256 | bytes 1 | tf_op jit(solution)/shard_map/heavy_rows/pallas_call | solution.py:244
  125.8 9.9 %collective-permute-done.22 = bf16[192,3072]{1,0:T(8,128)(2,1)S(1)} collective-permute-done((bf16[192,3072]{1,0:T(8,128)(2,1)S(1)}, bf16[192,3072]{1,0:T(8,128)(2,1)S(1)}, u32[]{:S(2)}, u32[]{:S(2)}) %collective-permute-start.22) | collective-permute-done | bytes 1179680 | tf_op jit(solution)/shard_map/ppermute | solution.py:93
  143.4 5.8 %collective-permute-done.24.refs_2_ = bf16[32,1536]{1,0:T(8,128)(2,1)S(1)} collective-permute-done((bf16[32,1536]{1,0:T(8,128)(2,1)S(1)}, bf16[32,1536]{1,0:T(8,128)(2,1)S(1)}, u32[]{:S(2)}, u32[]{:S(2)}) %collective-permute-start.24) | collective-permute-done | bytes 98336 | tf_op jit(solution)/shard_map/ppermute | solution.py:98
  149.2 4.4 %feed.1 = (f32[256,768]{1,0:T(8,128)S(1)}, f32[256,768]{1,0:T(8,128)S(1)}, bf16[256,1024]{1,0:T(8,128)(2,1)S(1)}, bf16[256,2048]{1,0:T(8,128)(2,1)S(1)}) custom-call(bf16[256,768]{1,0:T(8,128)(2,1)S(1)} %get-tuple-element.234.normed, bf16[256,768]{1,0:T(8,128)(2,1)S(1)} %copy-done.1, bf16[384,3072]{1,0:T(8,128)(2,1)S(1)} %pad_maximum_fusion.1.t0, ...), custom_call_target="tpu_custom_call" | custom-call | flops 4400000000 | bytes 1 | tf_op jit(solution)/shard_map/feed/pallas_call | solution.py:244
  157.4 12.7 %collective-permute-done.28 = bf16[384,1536]{1,0:T(8,128)(2,1)S(1)} collective-permute-done((bf16[384,1536]{1,0:T(8,128)(2,1)S(1)}, bf16[384,1536]{1,0:T(8,128)(2,1)S(1)}, u32[]{:S(2)}, u32[]{:S(2)}) %collective-permute-start.28) | collective-permute-done | bytes 1179680 | tf_op jit(solution)/shard_map/ppermute | solution.py:93
  170.2 5.9 %expert.1 = (bf16[128,1536]{1,0:T(8,128)(2,1)S(1)}, bf16[128,1536]{1,0:T(8,128)(2,1)S(1)}, bf16[384,1536]{1,0:T(8,128)(2,1)S(1)}, bf16[384,1536]{1,0:T(8,128)(2,1)S(1)}) custom-call(bf16[128,1536]{1,0:T(8,128)(2,1)S(1)} %stack.61.got0, bf16[128,1536]{1,0:T(8,128)(2,1)S(1)} %collective-permute-done.29.got1, bf16[768,768]{1,0:T(8,128)(2,1)S(1)} %copy-done.9, ...), custom_call_target="tpu_custom_call" | custom-call | flops 6000000000 | bytes 1 | tf_op jit(solution)/shard_map/expert/pallas_call | solution.py:244
  185.9 4.6 %collective-permute-done.33.refs_2_ = bf16[32,1536]{1,0:T(8,128)(2,1)S(1)} collective-permute-done((bf16[32,1536]{1,0:T(8,128)(2,1)S(1)}, bf16[32,1536]{1,0:T(8,128)(2,1)S(1)}, u32[]{:S(2)}, u32[]{:S(2)}) %collective-permute-start.33) | collective-permute-done | bytes 98336 | tf_op jit(solution)/shard_map/ppermute | solution.py:98
  194.7 4.0 %heavy_scores.1 = (bf16[32,768]{1,0:T(8,128)(2,1)S(1)}, bf16[32,768]{1,0:T(8,128)(2,1)S(1)}, bf16[1024,1536]{1,0:T(8,128)(2,1)S(1)}, f32[32,128]{1,0:T(8,128)S(1)}) custom-call(s32[32,1]{1,0:T(8,128)S(1)} %copy-done.10, s32[1,1024]{1,0:T(1,128)S(1)} %copy-done.12, f32[256,768]{1,0:T(8,128)S(1)} %get-tuple-element.288.grad_middle, ...), custom_call_target="tpu_custom_call" | custom-call | flops 4000000000 | bytes 1 | tf_op jit(solution)/shard_map/heavy_scores/pallas_call | solution.py:244
  198.7 10.9 %collective-permute-done.37.refs_4_.refs_5_.refs_6_.refs_7_ = bf16[192,1536]{1,0:T(8,128)(2,1)S(1)} collective-permute-done((bf16[192,1536]{1,0:T(8,128)(2,1)S(1)}, bf16[192,1536]{1,0:T(8,128)(2,1)S(1)}, u32[]{:S(2)}, u32[]{:S(2)}) %collective-permute-start.37) | collective-permute-done | bytes 589856 | tf_op jit(solution)/shard_map/ppermute | solution.py:93
  211.6 10.3 %heavy_weights.1 = (bf16[384,4608]{1,0:T(8,128)(2,1)S(1)}, bf16[384,4608]{1,0:T(8,128)(2,1)S(1)}, f32[32,768]{1,0:T(8,128)S(1)}, f32[8,768]{1,0:T(8,128)S(1)}) custom-call(f32[256,768]{1,0:T(8,128)S(1)} %get-tuple-element.288.grad_middle, bf16[32,768]{1,0:T(8,128)(2,1)S(1)} %get-tuple-element.227.routed, bf16[1024,768]{1,0:T(8,128)(2,1)S(1)} %get-tuple-element.275.keyed, ...), custom_call_target="tpu_custom_call" | custom-call | flops 10000000000 | bytes 1 | tf_op jit(solution)/shard_map/heavy_weights/pallas_call | solution.py:244
  227.5 4.0 %collective-permute-done.39.refs_1_ = bf16[48,1536]{1,0:T(8,128)(2,1)S(1)} collective-permute-done((bf16[48,1536]{1,0:T(8,128)(2,1)S(1)}, bf16[48,1536]{1,0:T(8,128)(2,1)S(1)}, u32[]{:S(2)}, u32[]{:S(2)}) %collective-permute-start.39) | collective-permute-done | bytes 147488 | tf_op jit(solution)/shard_map/ppermute | solution.py:98
  231.5 5.6 %collective-permute-done.40.refs_2_ = bf16[48,1536]{1,0:T(8,128)(2,1)S(1)} collective-permute-done((bf16[48,1536]{1,0:T(8,128)(2,1)S(1)}, bf16[48,1536]{1,0:T(8,128)(2,1)S(1)}, u32[]{:S(2)}, u32[]{:S(2)}) %collective-permute-start.40) | collective-permute-done | bytes 147488 | tf_op jit(solution)/shard_map/ppermute | solution.py:98
  237.3 5.6 %light_scores.1 = (bf16[256,512]{1,0:T(8,128)(2,1)S(1)}, bf16[512,1024]{1,0:T(8,128)(2,1)S(1)}) custom-call(s32[7]{0:T(128)S(1)} %copy-done.5, f32[256,768]{1,0:T(8,128)S(1)} %get-tuple-element.288.grad_middle, bf16[256,512]{1,0:T(8,128)(2,1)S(1)} %get-tuple-element.198.queries, bf16[512,1024]{1,0:T(8,128)(2,1)S(1)} %get-tuple-element.199.pairs, ...), custom_call_target="tpu_custom_call" | custom-call | flops 5600000000 | bytes 1 | tf_op jit(solution)/shard_map/light_scores/pallas_call | solution.py:244
  245.4 3.4 %light_weights.1 = (bf16[384,1664]{1,0:T(8,128)(2,1)S(1)}, bf16[384,1664]{1,0:T(8,128)(2,1)S(1)}, bf16[256,768]{1,0:T(8,128)(2,1)S(1)}, f32[256,768]{1,0:T(8,128)S(1)}) custom-call(bf16[512,768]{1,0:T(8,128)(2,1)S(1)} %prepare.1.raw, bf16[512,768]{1,0:T(8,128)(2,1)S(1)} %get-tuple-element.218.normed, bf16[256,512]{1,0:T(8,128)(2,1)S(1)} %get-tuple-element.294.grad_queries, ...), custom_call_target="tpu_custom_call" | custom-call | flops 3400000000 | bytes 1 | tf_op jit(solution)/shard_map/light_weights/pallas_call | solution.py:244
  258.0 7.7 %collective-permute-done.49.refs_2_ = bf16[24,3072]{1,0:T(8,128)(2,1)S(1)} collective-permute-done((bf16[24,3072]{1,0:T(8,128)(2,1)S(1)}, bf16[24,3072]{1,0:T(8,128)(2,1)S(1)}, u32[]{:S(2)}, u32[]{:S(2)}) %collective-permute-start.49) | collective-permute-done | bytes 147488 | tf_op jit(solution)/shard_map/ppermute | solution.py:98
  269.5 15.8 %collective-permute-done.52.refs_2_.refs_3_ = bf16[192,1664]{1,0:T(8,128)(2,1)S(1)} collective-permute-done((bf16[192,1664]{1,0:T(8,128)(2,1)S(1)}, bf16[192,1664]{1,0:T(8,128)(2,1)S(1)}, u32[]{:S(2)}, u32[]{:S(2)}) %collective-permute-start.52) | collective-permute-done | bytes 639008 | tf_op jit(solution)/shard_map/ppermute | solution.py:93
  286.8 3.4 %collective-permute-start.54 = (bf16[24,4608]{1,0:T(8,128)(2,1)S(1)}, bf16[24,4608]{1,0:T(8,128)(2,1)S(1)}, u32[]{:S(2)}, u32[]{:S(2)}) collective-permute-start(bf16[24,4608]{1,0:T(8,128)(2,1)S(1)} %get-tuple-element.325), channel_id=1, source_target_pairs={{0,1},{1,0},{2,3},{3,2},{4,5},{5,4},{6,7},{7,6},{8,9},{9,8},{10,11... | collective-permute-start | bytes 663560 | tf_op jit(solution)/shard_map/ppermute | solution.py:98
  293.9 4.6 %collective-permute-start.43 = (bf16[128,768]{1,0:T(8,128)(2,1)S(1)}, bf16[128,768]{1,0:T(8,128)(2,1)S(1)}, u32[]{:S(2)}, u32[]{:S(2)}) collective-permute-start(bf16[128,768]{1,0:T(8,128)(2,1)S(1)} %get-tuple-element.353), channel_id=1, source_target_pairs={{0,1},{1,2},{2,3},{3,4},{4,5},{5,6},{6,7},{7,8},{8,9},{9,10},{10,1... | collective-permute-start | bytes 589832 | tf_op jit(solution)/shard_map/ppermute | solution.py:1268
  299.7 9.8 %collective-permute-done.55.refs_2_ = bf16[24,4608]{1,0:T(8,128)(2,1)S(1)} collective-permute-done((bf16[24,4608]{1,0:T(8,128)(2,1)S(1)}, bf16[24,4608]{1,0:T(8,128)(2,1)S(1)}, u32[]{:S(2)}, u32[]{:S(2)}) %collective-permute-start.55) | collective-permute-done | bytes 221216 | tf_op jit(solution)/shard_map/ppermute | solution.py:98
  312.3 12.4 %collective-permute-done.58.refs_2_ = bf16[24,1664]{1,0:T(8,128)(2,1)S(1)} collective-permute-done((bf16[24,1664]{1,0:T(8,128)(2,1)S(1)}, bf16[24,1664]{1,0:T(8,128)(2,1)S(1)}, u32[]{:S(2)}, u32[]{:S(2)}) %collective-permute-start.58) | collective-permute-done | bytes 79904 | tf_op jit(solution)/shard_map/ppermute | solution.py:98
  (176 shorter events, 107.3 us)
Async XLA Ops:
  21.2 28.3 %collective-permute-start.9 = (bf16[192,1664]{1,0:T(8,128)(2,1)S(1)}, bf16[192,1664]{1,0:T(8,128)(2,1)S(1)}, u32[]{:S(2)}, u32[]{:S(2)}) collective-permute-start(bf16[192,1664]{1,0:T(8,128)(2,1)S(1)} %pad_maximum_fusion.7), channel_id=1, source_target_pairs={{0,8},{1,9},{2,10},{3,11},{4,20},{5,21},{6,22},{7,23},{8,0},{9,1},... | collective-permute-start | bytes 1916936 | tf_op jit(solution)/shard_map/ppermute | solution.py:93
  25.4 23.1 %collective-permute-start.5 = (bf16[24,4608]{1,0:T(8,128)(2,1)S(1)}, bf16[24,4608]{1,0:T(8,128)(2,1)S(1)}, u32[]{:S(2)}, u32[]{:S(2)}) collective-permute-start(bf16[24,4608]{1,0:T(8,128)(2,1)S(1)} %copy-done.6), channel_id=1, source_target_pairs={{0,2},{1,3},{2,0},{3,1},{4,6},{5,7},{6,4},{7,5},{8,10},{9,11},{10,... | collective-permute-start | bytes 663560 | tf_op jit(solution)/shard_map/ppermute | solution.py:98
  25.5 23.1 %collective-permute-start.4 = (bf16[24,4608]{1,0:T(8,128)(2,1)S(1)}, bf16[24,4608]{1,0:T(8,128)(2,1)S(1)}, u32[]{:S(2)}, u32[]{:S(2)}) collective-permute-start(bf16[24,4608]{1,0:T(8,128)(2,1)S(1)} %copy-done.6), channel_id=1, source_target_pairs={{0,1},{1,0},{2,3},{3,2},{4,5},{5,4},{6,7},{7,6},{8,9},{9,8},{10,11... | collective-permute-start | bytes 663560 | tf_op jit(solution)/shard_map/ppermute | solution.py:98
  27.2 21.5 %collective-permute-start.8 = (bf16[128,768]{1,0:T(8,128)(2,1)S(1)}, bf16[128,768]{1,0:T(8,128)(2,1)S(1)}, u32[]{:S(2)}, u32[]{:S(2)}) collective-permute-start(bf16[128,768]{1,0:T(8,128)(2,1)S(1)} %get-tuple-element.354), channel_id=1, source_target_pairs={{1,0},{2,1},{3,2},{4,3},{5,4},{6,5},{7,6},{8,7},{9,8},{10,9},{11,1... | collective-permute-start | bytes 589832 | tf_op jit(solution)/shard_map/ppermute | solution.py:943
  32.9 15.7 %collective-permute-start.7 = (bf16[128,768]{1,0:T(8,128)(2,1)S(1)}, bf16[128,768]{1,0:T(8,128)(2,1)S(1)}, u32[]{:S(2)}, u32[]{:S(2)}) collective-permute-start(bf16[128,768]{1,0:T(8,128)(2,1)S(1)} %get-tuple-element.355), channel_id=1, source_target_pairs={{0,1},{1,2},{2,3},{3,4},{4,5},{5,6},{6,7},{7,8},{8,9},{9,10},{10,1... | collective-permute-start | bytes 589832 | tf_op jit(solution)/shard_map/ppermute | solution.py:942
  62.9 22.6 %collective-permute-start.16 = (bf16[192,4608]{1,0:T(8,128)(2,1)S(1)}, bf16[192,4608]{1,0:T(8,128)(2,1)S(1)}, u32[]{:S(2)}, u32[]{:S(2)}) collective-permute-start(bf16[192,4608]{1,0:T(8,128)(2,1)S(1)} %pad_maximum_fusion.3), channel_id=1, source_target_pairs={{0,8},{1,9},{2,10},{3,11},{4,20},{5,21},{6,22},{7,23},{8,0},{9,1},... | collective-permute-start | bytes 5308424 | tf_op jit(solution)/shard_map/ppermute | solution.py:93
  85.9 24.1 %collective-permute-start.20 = (bf16[384,4608]{1,0:T(8,128)(2,1)S(1)}, bf16[384,4608]{1,0:T(8,128)(2,1)S(1)}, u32[]{:S(2)}, u32[]{:S(2)}) collective-permute-start(bf16[384,4608]{1,0:T(8,128)(2,1)S(1)} %pad_maximum_fusion.s0), channel_id=1, source_target_pairs={{0,4},{1,5},{2,6},{3,7},{4,0},{5,1},{6,2},{7,3},{8,12},{9,13},{10,... | collective-permute-start | bytes 10616840 | tf_op jit(solution)/shard_map/ppermute | solution.py:89
  95.4 13.9 %collective-permute-start.18 = (bf16[48,1536]{1,0:T(8,128)(2,1)S(1)}, bf16[48,1536]{1,0:T(8,128)(2,1)S(1)}, u32[]{:S(2)}, u32[]{:S(2)}) collective-permute-start(bf16[48,1536]{1,0:T(8,128)(2,1)S(1)} %get-tuple-element.215), channel_id=1, source_target_pairs={{0,2},{1,3},{2,0},{3,1},{4,6},{5,7},{6,4},{7,5},{8,10},{9,11},{10,... | collective-permute-start | bytes 442376 | tf_op jit(solution)/shard_map/ppermute | solution.py:98
  95.5 13.8 %collective-permute-start.19 = (bf16[48,1536]{1,0:T(8,128)(2,1)S(1)}, bf16[48,1536]{1,0:T(8,128)(2,1)S(1)}, u32[]{:S(2)}, u32[]{:S(2)}) collective-permute-start(bf16[48,1536]{1,0:T(8,128)(2,1)S(1)} %get-tuple-element.216), channel_id=1, source_target_pairs={{0,3},{1,2},{2,1},{3,0},{4,7},{5,6},{6,5},{7,4},{8,11},{9,10},{10,... | collective-permute-start | bytes 442376 | tf_op jit(solution)/shard_map/ppermute | solution.py:98
  119.4 16.3 %collective-permute-start.22 = (bf16[192,3072]{1,0:T(8,128)(2,1)S(1)}, bf16[192,3072]{1,0:T(8,128)(2,1)S(1)}, u32[]{:S(2)}, u32[]{:S(2)}) collective-permute-start(bf16[192,3072]{1,0:T(8,128)(2,1)S(1)} %pad_maximum_fusion.5), channel_id=1, source_target_pairs={{0,8},{1,9},{2,10},{3,11},{4,20},{5,21},{6,22},{7,23},{8,0},{9,1},... | collective-permute-start | bytes 3538952 | tf_op jit(solution)/shard_map/ppermute | solution.py:93
  135.8 13.4 %collective-permute-start.27 = (bf16[384,3072]{1,0:T(8,128)(2,1)S(1)}, bf16[384,3072]{1,0:T(8,128)(2,1)S(1)}, u32[]{:S(2)}, u32[]{:S(2)}) collective-permute-start(bf16[384,3072]{1,0:T(8,128)(2,1)S(1)} %pad_maximum_fusion.1.t0), channel_id=1, source_target_pairs={{0,4},{1,5},{2,6},{3,7},{4,0},{5,1},{6,2},{7,3},{8,12},{9,13},{10,... | collective-permute-start | bytes 7077896 | tf_op jit(solution)/shard_map/ppermute | solution.py:89
  140.3 13.4 %collective-permute-start.26 = (bf16[192,1536]{1,0:T(8,128)(2,1)S(1)}, bf16[192,1536]{1,0:T(8,128)(2,1)S(1)}, u32[]{:S(2)}, u32[]{:S(2)}) collective-permute-start(bf16[192,1536]{1,0:T(8,128)(2,1)S(1)} %stack.60), channel_id=1, source_target_pairs={{0,16},{1,17},{2,18},{3,19},{4,12},{5,13},{6,14},{7,15},{8,24},{9,... | collective-permute-start | bytes 1769480 | tf_op jit(solution)/shard_map/ppermute | solution.py:93
  153.8 16.3 %collective-permute-start.28 = (bf16[384,1536]{1,0:T(8,128)(2,1)S(1)}, bf16[384,1536]{1,0:T(8,128)(2,1)S(1)}, u32[]{:S(2)}, u32[]{:S(2)}) collective-permute-start(bf16[384,1536]{1,0:T(8,128)(2,1)S(1)} %pad_maximum_fusion.6), channel_id=1, source_target_pairs={{0,8},{1,9},{2,10},{3,11},{4,20},{5,21},{6,22},{7,23},{8,0},{9,1},... | collective-permute-start | bytes 3538952 | tf_op jit(solution)/shard_map/ppermute | solution.py:93
  156.8 20.9 %collective-permute-start.31 = (bf16[384,3072]{1,0:T(8,128)(2,1)S(1)}, bf16[384,3072]{1,0:T(8,128)(2,1)S(1)}, u32[]{:S(2)}, u32[]{:S(2)}) collective-permute-start(bf16[384,3072]{1,0:T(8,128)(2,1)S(1)} %get-tuple-element.239), channel_id=1, source_target_pairs={{0,4},{1,5},{2,6},{3,7},{4,0},{5,1},{6,2},{7,3},{8,12},{9,13},{10,... | collective-permute-start | bytes 7077896 | tf_op jit(solution)/shard_map/ppermute | solution.py:89
  156.9 13.3 %collective-permute-start.29 = (bf16[128,1536]{1,0:T(8,128)(2,1)S(1)}, bf16[128,1536]{1,0:T(8,128)(2,1)S(1)}, u32[]{:S(2)}, u32[]{:S(2)}) collective-permute-start(bf16[128,1536]{1,0:T(8,128)(2,1)S(1)} %stack.61.got0), channel_id=1, source_target_pairs={{0,4},{1,5},{2,6},{3,7},{4,0},{5,1},{6,2},{7,3},{8,12},{9,13},{10,... | collective-permute-start | bytes 1179656 | tf_op jit(solution)/shard_map/ppermute | solution.py:89
  176.1 17.2 %collective-permute-start.36 = (bf16[384,1536]{1,0:T(8,128)(2,1)S(1)}, bf16[384,1536]{1,0:T(8,128)(2,1)S(1)}, u32[]{:S(2)}, u32[]{:S(2)}) collective-permute-start(bf16[384,1536]{1,0:T(8,128)(2,1)S(1)} %get-tuple-element.262), channel_id=1, source_target_pairs={{0,8},{1,9},{2,10},{3,11},{4,20},{5,21},{6,22},{7,23},{8,0},{9,1},... | collective-permute-start | bytes 3538952 | tf_op jit(solution)/shard_map/ppermute | solution.py:93
  178.3 33.0 %collective-permute-start.35 = (bf16[192,3072]{1,0:T(8,128)(2,1)S(1)}, bf16[192,3072]{1,0:T(8,128)(2,1)S(1)}, u32[]{:S(2)}, u32[]{:S(2)}) collective-permute-start(bf16[192,3072]{1,0:T(8,128)(2,1)S(1)} %get-tuple-element.260), channel_id=1, source_target_pairs={{0,8},{1,9},{2,10},{3,11},{4,20},{5,21},{6,22},{7,23},{8,0},{9,1},... | collective-permute-start | bytes 3538952 | tf_op jit(solution)/shard_map/ppermute | solution.py:93
  193.6 16.0 %collective-permute-start.37 = (bf16[192,1536]{1,0:T(8,128)(2,1)S(1)}, bf16[192,1536]{1,0:T(8,128)(2,1)S(1)}, u32[]{:S(2)}, u32[]{:S(2)}) collective-permute-start(bf16[192,1536]{1,0:T(8,128)(2,1)S(1)} %get-tuple-element.265), channel_id=1, source_target_pairs={{0,16},{1,17},{2,18},{3,19},{4,12},{5,13},{6,14},{7,15},{8,24},{9,... | collective-permute-start | bytes 1769480 | tf_op jit(solution)/shard_map/ppermute | solution.py:93
  222.0 21.0 %collective-permute-start.42 = (bf16[384,4608]{1,0:T(8,128)(2,1)S(1)}, bf16[384,4608]{1,0:T(8,128)(2,1)S(1)}, u32[]{:S(2)}, u32[]{:S(2)}) collective-permute-start(bf16[384,4608]{1,0:T(8,128)(2,1)S(1)} %get-tuple-element.280), channel_id=1, source_target_pairs={{0,4},{1,5},{2,6},{3,7},{4,0},{5,1},{6,2},{7,3},{8,12},{9,13},{10,... | collective-permute-start | bytes 10616840 | tf_op jit(solution)/shard_map/ppermute | solution.py:89
  222.0 15.1 %collective-permute-start.38 = (bf16[96,3072]{1,0:T(8,128)(2,1)S(1)}, bf16[96,3072]{1,0:T(8,128)(2,1)S(1)}, u32[]{:S(2)}, u32[]{:S(2)}) collective-permute-start(bf16[96,3072]{1,0:T(8,128)(2,1)S(1)} %get-tuple-element.274), channel_id=1, source_target_pairs={{0,16},{1,17},{2,18},{3,19},{4,12},{5,13},{6,14},{7,15},{8,24},{9,... | collective-permute-start | bytes 1769480 | tf_op jit(solution)/shard_map/ppermute | solution.py:93
  223.1 14.0 %collective-permute-start.40 = (bf16[48,1536]{1,0:T(8,128)(2,1)S(1)}, bf16[48,1536]{1,0:T(8,128)(2,1)S(1)}, u32[]{:S(2)}, u32[]{:S(2)}) collective-permute-start(bf16[48,1536]{1,0:T(8,128)(2,1)S(1)} %get-tuple-element.283), channel_id=1, source_target_pairs={{0,2},{1,3},{2,0},{3,1},{4,6},{5,7},{6,4},{7,5},{8,10},{9,11},{10,... | collective-permute-start | bytes 442376 | tf_op jit(solution)/shard_map/ppermute | solution.py:98
  243.8 22.7 %collective-permute-start.45 = (bf16[192,4608]{1,0:T(8,128)(2,1)S(1)}, bf16[192,4608]{1,0:T(8,128)(2,1)S(1)}, u32[]{:S(2)}, u32[]{:S(2)}) collective-permute-start(bf16[192,4608]{1,0:T(8,128)(2,1)S(1)} %get-tuple-element.300), channel_id=1, source_target_pairs={{0,8},{1,9},{2,10},{3,11},{4,20},{5,21},{6,22},{7,23},{8,0},{9,1},... | collective-permute-start | bytes 5308424 | tf_op jit(solution)/shard_map/ppermute | solution.py:93
  251.8 14.0 %collective-permute-start.49 = (bf16[24,3072]{1,0:T(8,128)(2,1)S(1)}, bf16[24,3072]{1,0:T(8,128)(2,1)S(1)}, u32[]{:S(2)}, u32[]{:S(2)}) collective-permute-start(bf16[24,3072]{1,0:T(8,128)(2,1)S(1)} %get-tuple-element.310), channel_id=1, source_target_pairs={{0,2},{1,3},{2,0},{3,1},{4,6},{5,7},{6,4},{7,5},{8,10},{9,11},{10,... | collective-permute-start | bytes 442376 | tf_op jit(solution)/shard_map/ppermute | solution.py:98
  252.3 13.4 %collective-permute-start.50 = (bf16[24,3072]{1,0:T(8,128)(2,1)S(1)}, bf16[24,3072]{1,0:T(8,128)(2,1)S(1)}, u32[]{:S(2)}, u32[]{:S(2)}) collective-permute-start(bf16[24,3072]{1,0:T(8,128)(2,1)S(1)} %get-tuple-element.311), channel_id=1, source_target_pairs={{0,3},{1,2},{2,1},{3,0},{4,7},{5,6},{6,5},{7,4},{8,11},{9,10},{10,... | collective-permute-start | bytes 442376 | tf_op jit(solution)/shard_map/ppermute | solution.py:98
  266.9 19.7 %collective-permute-start.51 = (bf16[96,4608]{1,0:T(8,128)(2,1)S(1)}, bf16[96,4608]{1,0:T(8,128)(2,1)S(1)}, u32[]{:S(2)}, u32[]{:S(2)}) collective-permute-start(bf16[96,4608]{1,0:T(8,128)(2,1)S(1)} %get-tuple-element.315), channel_id=1, source_target_pairs={{0,16},{1,17},{2,18},{3,19},{4,12},{5,13},{6,14},{7,15},{8,24},{9,... | collective-permute-start | bytes 2654216 | tf_op jit(solution)/shard_map/ppermute | solution.py:93
  268.0 17.3 %collective-permute-start.52 = (bf16[192,1664]{1,0:T(8,128)(2,1)S(1)}, bf16[192,1664]{1,0:T(8,128)(2,1)S(1)}, u32[]{:S(2)}, u32[]{:S(2)}) collective-permute-start(bf16[192,1664]{1,0:T(8,128)(2,1)S(1)} %get-tuple-element.316), channel_id=1, source_target_pairs={{0,8},{1,9},{2,10},{3,11},{4,20},{5,21},{6,22},{7,23},{8,0},{9,1},... | collective-permute-start | bytes 1916936 | tf_op jit(solution)/shard_map/ppermute | solution.py:93
  290.2 19.3 %collective-permute-start.55 = (bf16[24,4608]{1,0:T(8,128)(2,1)S(1)}, bf16[24,4608]{1,0:T(8,128)(2,1)S(1)}, u32[]{:S(2)}, u32[]{:S(2)}) collective-permute-start(bf16[24,4608]{1,0:T(8,128)(2,1)S(1)} %get-tuple-element.326), channel_id=1, source_target_pairs={{0,2},{1,3},{2,0},{3,1},{4,6},{5,7},{6,4},{7,5},{8,10},{9,11},{10,... | collective-permute-start | bytes 663560 | tf_op jit(solution)/shard_map/ppermute | solution.py:98
  290.3 19.2 %collective-permute-start.56 = (bf16[24,4608]{1,0:T(8,128)(2,1)S(1)}, bf16[24,4608]{1,0:T(8,128)(2,1)S(1)}, u32[]{:S(2)}, u32[]{:S(2)}) collective-permute-start(bf16[24,4608]{1,0:T(8,128)(2,1)S(1)} %get-tuple-element.327), channel_id=1, source_target_pairs={{0,3},{1,2},{2,1},{3,0},{4,7},{5,6},{6,5},{7,4},{8,11},{9,10},{10,... | collective-permute-start | bytes 663560 | tf_op jit(solution)/shard_map/ppermute | solution.py:98
  292.6 33.5 %collective-permute-start.44 = (bf16[128,768]{1,0:T(8,128)(2,1)S(1)}, bf16[128,768]{1,0:T(8,128)(2,1)S(1)}, u32[]{:S(2)}, u32[]{:S(2)}) collective-permute-start(bf16[128,768]{1,0:T(8,128)(2,1)S(1)} %get-tuple-element.352), channel_id=1, source_target_pairs={{1,0},{2,1},{3,2},{4,3},{5,4},{6,5},{7,6},{8,7},{9,8},{10,9},{11,1... | collective-permute-start | bytes 589832 | tf_op jit(solution)/shard_map/ppermute | solution.py:1267
  293.9 32.2 %collective-permute-start.43 = (bf16[128,768]{1,0:T(8,128)(2,1)S(1)}, bf16[128,768]{1,0:T(8,128)(2,1)S(1)}, u32[]{:S(2)}, u32[]{:S(2)}) collective-permute-start(bf16[128,768]{1,0:T(8,128)(2,1)S(1)} %get-tuple-element.353), channel_id=1, source_target_pairs={{0,1},{1,2},{2,3},{3,4},{4,5},{5,6},{6,7},{7,8},{8,9},{9,10},{10,1... | collective-permute-start | bytes 589832 | tf_op jit(solution)/shard_map/ppermute | solution.py:1268
  309.5 15.2 %collective-permute-start.58 = (bf16[24,1664]{1,0:T(8,128)(2,1)S(1)}, bf16[24,1664]{1,0:T(8,128)(2,1)S(1)}, u32[]{:S(2)}, u32[]{:S(2)}) collective-permute-start(bf16[24,1664]{1,0:T(8,128)(2,1)S(1)} %get-tuple-element.334), channel_id=1, source_target_pairs={{0,2},{1,3},{2,0},{3,1},{4,6},{5,7},{6,4},{7,5},{8,10},{9,11},{10,... | collective-permute-start | bytes 239624 | tf_op jit(solution)/shard_map/ppermute | solution.py:98
  309.5 15.2 %collective-permute-start.59 = (bf16[24,1664]{1,0:T(8,128)(2,1)S(1)}, bf16[24,1664]{1,0:T(8,128)(2,1)S(1)}, u32[]{:S(2)}, u32[]{:S(2)}) collective-permute-start(bf16[24,1664]{1,0:T(8,128)(2,1)S(1)} %get-tuple-element.335), channel_id=1, source_target_pairs={{0,3},{1,2},{2,1},{3,0},{4,7},{5,6},{6,5},{7,4},{8,11},{9,10},{10,... | collective-permute-start | bytes 239624 | tf_op jit(solution)/shard_map/ppermute | solution.py:98
  (42 other events, 385.9 us)
